TPU v7x, 128 devices: a whole 4x4x4 slice. The times are simulated.
128 devices in a mesh: gx: 32 (over y_lo, x, z), gy: 4 (over y_hi, core).
Axes of the slice: x: 4, y: 4 (y_hi: 2, y_lo: 2; y = y_hi * 2 + y_lo), z: 4, core: 2. Of those that a mesh axis runs over, the one named last changes fastest.
Arguments:
- electric: float32 [3, 128, 96, 512], P(None, 'gx', None, 'gy'), may hold values from -6 to 6
- magnetic: float32 [3, 128, 96, 512], P(None, 'gx', None, 'gy'), may hold values from -6 to 6
- polarization: float32 [3, 128, 96, 512], P(None, 'gx', None, 'gy'), may hold values from -6 to 6
- current: float32 [3, 128, 96, 512], P(None, 'gx', None, 'gy'), may hold values from -6 to 6
- inversion: float32 [128, 96, 512], P('gx', None, 'gy'), may hold values from -1 to 1
- gain_mask: int32 [128, 96, 512], P('gx', None, 'gy'), may hold values 0 or 1
- pump_region: int32 [128, 96, 512], P('gx', None, 'gy'), may hold values from 0 to 7
- pump_level: float32 [8], replicated, may hold values from -0.5 to 2
Outputs:
- final_field: float32 [3, 128, 96, 512], P(None, 'gx', None, 'gy')
- far_field: float32 [64, 16, 512], P('gx', 'gy')
All inputs are finite; a program needn't handle non-finite values. No bound on the sum of `gain_mask` on one device may be relied on, other than what follows from the above.
Results may differ from a plain program's by a relative error of at most 0.0003.
Values sent between devices are 32-bit elements; how exact they have to be, the bound alone decides.
A program may use at most 64 MiB of HBM per device.

v0:
```python
import math

import jax
import jax.numpy as jnp
from jax import lax
from jax.sharding import PartitionSpec as P

STEPS = 4
NF = 16
NUX = 64
NUY = 64


time_step = 0.5
damping = 0.4
omega_zero = 1.0
coupling = 1.0
saturation = 0.5
recovery = 0.8
freq_base = 0.6
freq_step = 0.05
spread_cosine = 0.75


def extended(cells, sides, width):
    for axis, dim in sides:
        count = lax.axis_size(axis)
        ends = count - 1
        head = lax.slice_in_dim(cells, 0, width, axis=dim)
        tail = lax.slice_in_dim(cells, cells.shape[dim] - width, cells.shape[dim], axis=dim)
        cells = jnp.concatenate(
            [
                lax.ppermute(tail, axis, [(i, (i + 1) % count) for i in range(ends)]),
                cells,
                lax.ppermute(head, axis, [((i + 1) % count, i) for i in range(ends)]),
            ],
            axis=dim,
        )
    return cells


def magnetic_update(magnetic, electric_ext):
    field_x, field_y, field_z = (electric_ext[0], electric_ext[1], electric_ext[2])

    def magnetic_central(value):
        return value[:-1, :, :-1]

    def delta_x(value):
        return value[1:, :, :-1] - value[:-1, :, :-1]

    def delta_y(value):
        return value[:-1, :, 1:] - value[:-1, :, :-1]

    def delta_z(value):
        middle = magnetic_central(value)
        shifted = jnp.concatenate([middle[:, 1:, :], jnp.zeros_like(middle[:, :1, :])], axis=1)
        return shifted - middle

    curl = jnp.stack(
        [
            delta_y(field_z) - delta_z(field_y),
            delta_z(field_x) - delta_x(field_z),
            delta_x(field_y) - delta_y(field_x),
        ]
    )
    return magnetic - time_step * curl


def electric_curl(magnetic_ext):
    field_x, field_y, field_z = (magnetic_ext[0], magnetic_ext[1], magnetic_ext[2])

    def electric_central(value):
        return value[1:, :, 1:]

    def delta_x(value):
        return value[1:, :, 1:] - value[:-1, :, 1:]

    def delta_y(value):
        return value[1:, :, 1:] - value[1:, :, :-1]

    def delta_z(value):
        middle = electric_central(value)
        shifted = jnp.concatenate([jnp.zeros_like(middle[:, :1, :]), middle[:, :-1, :]], axis=1)
        return middle - shifted

    return jnp.stack(
        [
            delta_y(field_z) - delta_z(field_y),
            delta_z(field_x) - delta_x(field_z),
            delta_x(field_y) - delta_y(field_x),
        ]
    )


def bloch_update(electric, curl_field, polarization, current, inversion, gain_cells, pump_rate):
    driven = (1.0 - 0.5 * damping * time_step) * current + time_step * (
        coupling * inversion[None] * electric - omega_zero * omega_zero * polarization
    )
    current_new = gain_cells[None] * driven / (1.0 + 0.5 * damping * time_step)
    polar_new = polarization + time_step * current_new
    electric_new = electric + time_step * (curl_field - current_new)
    absorbed = 0.5 * jnp.sum((electric + electric_new) * current_new, axis=0)
    inversion_new = inversion + time_step * (
        recovery * (pump_rate - inversion) - saturation * absorbed
    )
    return (electric_new, polar_new, current_new, inversion_new)


def frequencies_from(first, count):
    return freq_base + freq_step * (first + jnp.arange(count)).astype(jnp.float32)


def directions(count, first, rows):
    places = (first + jnp.arange(rows)).astype(jnp.float32)
    return spread_cosine * (2.0 * places - (count - 1)) / (count - 1)


def accumulate(real, imag, top, moment, count):
    phase = frequencies_from(0, count) * moment
    real = real + (time_step * jnp.cos(phase))[:, None, None, None] * top[None]
    imag = imag + (-time_step * jnp.sin(phase))[:, None, None, None] * top[None]
    return (real, imag)


def product(form, left, right):
    return jnp.einsum(
        form, left, right, precision=lax.Precision.HIGHEST, preferred_element_type=jnp.float32
    )


def contract_y(spectra, wavenumber, places):
    cosines = directions(NUY, 0, NUY)
    phase = (wavenumber[:, None] * cosines[None, :])[:, :, None] * places[None, None, :]
    cos_table = jnp.cos(phase)
    sin_table = jnp.sin(phase)
    real_part = spectra[:, :4]
    imag_part = spectra[:, 4:]
    inner_real = product("fcxy,fby->fcxb", real_part, cos_table) - product(
        "fcxy,fby->fcxb", imag_part, sin_table
    )
    inner_imag = product("fcxy,fby->fcxb", real_part, sin_table) + product(
        "fcxy,fby->fcxb", imag_part, cos_table
    )
    return jnp.concatenate([inner_real, inner_imag], axis=1)


def contract_x(inner, wavenumber, stations, first, rows):
    cosines = directions(NUX, first, rows)
    phase = (wavenumber[:, None] * cosines[None, :])[:, :, None] * stations[None, None, :]
    cos_rows = jnp.cos(phase)
    sin_rows = jnp.sin(phase)
    inner_real = inner[:, :4]
    inner_imag = inner[:, 4:]
    outer_real = product("fax,fcxb->afcb", cos_rows, inner_real) - product(
        "fax,fcxb->afcb", sin_rows, inner_imag
    )
    outer_imag = product("fax,fcxb->afcb", sin_rows, inner_real) + product(
        "fax,fcxb->afcb", cos_rows, inner_imag
    )
    joined = jnp.concatenate([outer_real, outer_imag], axis=2)
    return joined.reshape(rows, joined.shape[1], 8 * NUY)


def local(electric, magnetic, polarization, current, inversion, gain_mask, pump_region, pump_level):
    cells_x = electric.shape[1]
    cells_y = electric.shape[3]
    count_x = lax.axis_size("gx")
    count_y = lax.axis_size("gy")
    total_x = cells_x * count_x
    total_y = cells_y * count_y
    freq_local = NF // count_y
    index_x = lax.axis_index("gx")
    index_y = lax.axis_index("gy")
    gain_cells = gain_mask.astype(jnp.float32)
    pump_rate = jnp.zeros(pump_region.shape, jnp.float32)
    for region in range(pump_level.shape[0]):
        pump_rate = jnp.where(pump_region == region, pump_level[region], pump_rate)
    plane = (NF, 2, cells_x, cells_y)
    h_real = jnp.zeros(plane, jnp.float32)
    h_imag = jnp.zeros(plane, jnp.float32)
    e_real = jnp.zeros(plane, jnp.float32)
    e_imag = jnp.zeros(plane, jnp.float32)
    rows_keep = jnp.where(jnp.arange(cells_x + 1) == 0, (index_x > 0).astype(jnp.float32), 1.0)
    cols_keep = jnp.where(jnp.arange(cells_y + 1) == 0, (index_y > 0).astype(jnp.float32), 1.0)
    keeper = rows_keep[None, :, None, None] * cols_keep[None, None, None, :]
    for iteration in range(STEPS):
        stacked = jnp.concatenate([electric, magnetic], axis=0)
        padded = extended(stacked, (("gx", 1), ("gy", 3)), 1)
        magnetic_ext = magnetic_update(padded[3:, :-1, :, :-1], padded[:3]) * keeper
        magnetic = magnetic_ext[:, 1:, :, 1:]
        top_h = jnp.stack([-magnetic[1, :, -1, :], magnetic[0, :, -1, :]])
        h_real, h_imag = accumulate(h_real, h_imag, top_h, (iteration + 0.5) * time_step, NF)
        electric, polarization, current, inversion = bloch_update(
            electric,
            electric_curl(magnetic_ext),
            polarization,
            current,
            inversion,
            gain_cells,
            pump_rate,
        )
        top_e = jnp.stack([electric[1, :, -1, :], -electric[0, :, -1, :]])
        e_real, e_imag = accumulate(e_real, e_imag, top_e, (iteration + 1.0) * time_step, NF)
    spectra = jnp.concatenate([h_real, e_real, h_imag, e_imag], axis=1)
    own_wave = frequencies_from(index_y * freq_local, freq_local)
    stations = (index_x * cells_x + jnp.arange(cells_x)).astype(jnp.float32) - total_x / 2
    places = jnp.arange(total_y).astype(jnp.float32) - total_y / 2
    inner = contract_y(
        lax.all_to_all(spectra, "gy", split_axis=0, concat_axis=3, tiled=True), own_wave, places
    )
    scale = 1.0 / math.sqrt(total_x * total_y)
    rows = NUX // count_x
    whole = lax.psum(contract_x(inner, own_wave, stations, 0, NUX) * scale, "gx")
    far_field = lax.dynamic_slice_in_dim(whole, index_x * rows, rows, 0)
    return (electric, far_field)


def solution(mesh):
    return jax.shard_map(
        local,
        mesh=mesh,
        in_specs=(
            P(None, "gx", None, "gy"),
            P(None, "gx", None, "gy"),
            P(None, "gx", None, "gy"),
            P(None, "gx", None, "gy"),
            P("gx", None, "gy"),
            P("gx", None, "gy"),
            P("gx", None, "gy"),
            P(),
        ),
        out_specs=(P(None, "gx", None, "gy"), P("gx", "gy", None)),
        check_vma=False,
    )
```

profile of v0, /device:TPU:0, one launch (start us, length us, event | category | flops | bytes accessed | tf_op | source)
XLA Modules:
  0.0 562.5 jit_solution(6803137601582146272)
XLA Ops:
  10.6 4.0 collective-permute-start
  26.6 2.1 fusion.127
  28.7 2.8 copy.235
  41.7 2.8 copy.237
  44.5 3.5 maximum_bitcast_fusion.7
  53.2 2.6 multiply_reduce_fusion.2
  57.0 3.7 collective-permute-start.4
  62.4 5.7 %fusion.96 = f32[4,96,128]{2,1,0:T(8,128)} fusion(f32[4,96,128]{2,1,0:T(8,128)S(1)} %copy-done.53, f32[4,96,128]{2,0,1:T(4,128)S(1)} %get-tuple-element.14, f32[]{:T(128)} %bitcast.31, s32[4,96,128]{2,1,0:T(8,128)S(1)} %copy-done.46, f32[]{:T(128)} %bitcast.30, f32[]{:T(128)} %bitcast.29, f32[]{:T(128)} %bitcast.28, f32[]{:T(128)} %bitcast.27, f32[]{:T(128)} %bitcast.26, ...), kind=kLoop, calls=%fused_computation.217 | loop fusion | flops 1081344 | bytes 786464 | tf_op jit(solution)/shard_map/add | solution.py:103
  73.3 2.8 copy.246
  77.3 5.4 collective-permute-start.6
  89.0 2.8 copy.248
  91.8 3.5 maximum_bitcast_fusion.5
  102.5 4.1 collective-permute-start.8
  108.7 5.7 %fusion.93 = f32[4,96,128]{2,1,0:T(8,128)} fusion(f32[4,96,128]{2,1,0:T(8,128)S(1)} %copy-done.50, f32[4,96,128]{2,0,1:T(4,128)S(1)} %get-tuple-element.30, f32[]{:T(128)} %bitcast.31, s32[4,96,128]{2,1,0:T(8,128)S(1)} %copy-done.47, f32[]{:T(128)} %bitcast.30, f32[]{:T(128)} %bitcast.29, f32[]{:T(128)} %bitcast.28, f32[]{:T(128)} %bitcast.27, f32[]{:T(128)} %bitcast.26, ...), kind=kLoop, calls=%fused_computation.213 | loop fusion | flops 1081344 | bytes 786464 | tf_op jit(solution)/shard_map/add | solution.py:103
  119.1 2.8 copy.255
  123.1 5.9 %collective-permute-start.10 = (f32[6,6,96,1]{2,3,1,0:T(1,128)}, f32[6,6,96,1]{2,3,1,0:T(1,128)}, u32[]{:S(2)}, u32[]{:S(2)}) collective-permute-start(f32[6,6,96,1]{2,3,1,0:T(1,128)} %copy.253), channel_id=1, source_target_pairs={{0,1},{1,2},{2,3},{4,5},{5,6},{6,7},{8,9},{9,10},{10,11},{12,13},{... | collective-permute-start | bytes 41480 | tf_op jit(solution)/shard_map/ppermute | solution.py:33
  136.1 2.8 copy.257
  138.9 3.5 maximum_bitcast_fusion.3
  150.4 4.8 collective-permute-start.12
  157.4 5.7 %fusion.90 = f32[4,96,128]{2,1,0:T(8,128)} fusion(f32[4,96,128]{2,1,0:T(8,128)S(1)} %copy-done.49, f32[4,96,128]{2,0,1:T(4,128)S(1)} %get-tuple-element.12, f32[]{:T(128)} %bitcast.31, s32[4,96,128]{2,1,0:T(8,128)S(1)} %copy-done.48, f32[]{:T(128)} %bitcast.30, f32[]{:T(128)} %bitcast.29, f32[]{:T(128)} %bitcast.28, f32[]{:T(128)} %bitcast.27, f32[]{:T(128)} %bitcast.26, ...), kind=kLoop, calls=%fused_computation.209 | loop fusion | flops 1081344 | bytes 786464 | tf_op jit(solution)/shard_map/add | solution.py:103
  163.1 3.6 collective-permute-done.13
  170.4 2.8 copy.262
  174.3 3.9 collective-permute-start.14
  185.3 2.8 copy.264
  188.1 3.5 maximum_bitcast_fusion.1
  200.0 7.3 %all-to-all-start = ((f32[16,8,4,128]{3,1,2,0:T(8,128)}), f32[16,8,4,128]{3,1,2,0:T(8,128)S(1)}, u32[]{:S(2)}, u32[]{:S(2)}) async-start(f32[16,8,4,128]{3,1,2,0:T(8,128)} %pad_maximum_fusion.44), calls=%async_computation | async-start | bytes 524288 | tf_op jit(solution)/shard_map/all_to_all | solution.py:209
  207.6 7.2 %all-to-all-done = f32[16,8,4,128]{3,1,2,0:T(8,128)S(1)} async-done(((f32[16,8,4,128]{3,1,2,0:T(8,128)}), f32[16,8,4,128]{3,1,2,0:T(8,128)S(1)}, u32[]{:S(2)}, u32[]{:S(2)}) %all-to-all-start) | async-done | bytes 262176 | tf_op jit(solution)/shard_map/all_to_all | solution.py:209
  215.1 2.6 fusion.50
  217.7 2.6 fusion.53
  220.3 2.6 convolution_subtract_fusion.1
  225.1 2.6 convolution_add_fusion.1
  232.1 321.8 %all-reduce.18.cloned.1.call-done = f32[64,4,512]{2,1,0:T(4,128)} async-done(((f32[64,4,512]{2,1,0:T(4,128)}), f32[64,4,512]{2,1,0:T(4,128)}) %all-reduce.18.cloned.1.call-update) | async-done | bytes 524304 | tf_op jit(solution)/shard_map/psum | solution.py:213
  (305 shorter events, 106.4 us)
Async XLA Ops:
  7.2 15.4 %copy-start.55 = (f32[8]{0:T(128)S(1)}, f32[8]{0:T(128)}, u32[]{:S(2)}) copy-start(f32[8]{0:T(128)} %param.15) | copy-start | bytes 100
  10.6 12.7 %collective-permute-start = (f32[6,1,96,128]{3,1,2,0:T(1,128)S(1)}, f32[6,1,96,128]{3,1,2,0:T(1,128)S(1)}, u32[]{:S(2)}, u32[]{:S(2)}) collective-permute-start(f32[6,1,96,128]{3,1,2,0:T(1,128)S(1)} %get-tuple-element.65), channel_id=1, source_target_pairs={{0,4},{4,8},{8,12},{12,16},{16,20},{20,24},{24,28},{28,32},{32,36}... | collective-permute-start | bytes 884744 | tf_op jit(solution)/shard_map/ppermute | solution.py:33
  14.6 10.5 %collective-permute-start.1 = (f32[6,1,96,128]{3,1,2,0:T(1,128)S(1)}, f32[6,1,96,128]{3,1,2,0:T(1,128)S(1)}, u32[]{:S(2)}, u32[]{:S(2)}) collective-permute-start(f32[6,1,96,128]{3,1,2,0:T(1,128)S(1)} %get-tuple-element.66), channel_id=1, source_target_pairs={{4,0},{8,4},{12,8},{16,12},{20,16},{24,20},{28,24},{32,28},{36,32}... | collective-permute-start | bytes 884744 | tf_op jit(solution)/shard_map/ppermute | solution.py:35
  32.8 7.4 %collective-permute-start.2 = (f32[6,6,96,1]{2,3,1,0:T(1,128)}, f32[6,6,96,1]{2,3,1,0:T(1,128)}, u32[]{:S(2)}, u32[]{:S(2)}) collective-permute-start(f32[6,6,96,1]{2,3,1,0:T(1,128)} %copy.233), channel_id=1, source_target_pairs={{0,1},{1,2},{2,3},{4,5},{5,6},{6,7},{8,9},{9,10},{10,11},{12,13},{... | collective-permute-start | bytes 41480 | tf_op jit(solution)/shard_map/ppermute | solution.py:33
  34.6 7.0 %collective-permute-start.3 = (f32[6,6,96,1]{2,3,1,0:T(1,128)}, f32[6,6,96,1]{2,3,1,0:T(1,128)}, u32[]{:S(2)}, u32[]{:S(2)}) collective-permute-start(f32[6,6,96,1]{2,3,1,0:T(1,128)} %copy.235), channel_id=1, source_target_pairs={{1,0},{2,1},{3,2},{5,4},{6,5},{7,6},{9,8},{10,9},{11,10},{13,12},{... | collective-permute-start | bytes 41480 | tf_op jit(solution)/shard_map/ppermute | solution.py:35
  53.2 9.1 %copy-start.46 = (s32[4,96,128]{2,1,0:T(8,128)S(1)}, s32[4,96,128]{2,1,0:T(8,128)}, u32[]{:S(2)}) copy-start(s32[4,96,128]{2,1,0:T(8,128)} %param.14) | copy-start | bytes 589828
  53.2 9.1 %copy-start.53 = (f32[4,96,128]{2,1,0:T(8,128)S(1)}, f32[4,96,128]{2,1,0:T(8,128)}, u32[]{:S(2)}) copy-start(f32[4,96,128]{2,1,0:T(8,128)} %param.12) | copy-start | bytes 589828
  57.0 11.1 %collective-permute-start.4 = (f32[6,1,96,128]{3,1,2,0:T(1,128)S(1)}, f32[6,1,96,128]{3,1,2,0:T(1,128)S(1)}, u32[]{:S(2)}, u32[]{:S(2)}) collective-permute-start(f32[6,1,96,128]{3,1,2,0:T(1,128)S(1)} %get-tuple-element.63), channel_id=1, source_target_pairs={{0,4},{4,8},{8,12},{12,16},{16,20},{20,24},{24,28},{28,32},{32,36}... | collective-permute-start | bytes 884744 | tf_op jit(solution)/shard_map/ppermute | solution.py:33
  60.6 9.0 %collective-permute-start.5 = (f32[6,1,96,128]{3,1,2,0:T(1,128)S(1)}, f32[6,1,96,128]{3,1,2,0:T(1,128)S(1)}, u32[]{:S(2)}, u32[]{:S(2)}) collective-permute-start(f32[6,1,96,128]{3,1,2,0:T(1,128)S(1)} %get-tuple-element.64), channel_id=1, source_target_pairs={{4,0},{8,4},{12,8},{16,12},{20,16},{24,20},{28,24},{32,28},{36,32}... | collective-permute-start | bytes 884744 | tf_op jit(solution)/shard_map/ppermute | solution.py:35
  77.3 9.1 %collective-permute-start.6 = (f32[6,6,96,1]{2,3,1,0:T(1,128)}, f32[6,6,96,1]{2,3,1,0:T(1,128)}, u32[]{:S(2)}, u32[]{:S(2)}) collective-permute-start(f32[6,6,96,1]{2,3,1,0:T(1,128)} %copy.244), channel_id=1, source_target_pairs={{0,1},{1,2},{2,3},{4,5},{5,6},{6,7},{8,9},{9,10},{10,11},{12,13},{... | collective-permute-start | bytes 41480 | tf_op jit(solution)/shard_map/ppermute | solution.py:33
  82.7 6.3 %collective-permute-start.7 = (f32[6,6,96,1]{2,3,1,0:T(1,128)}, f32[6,6,96,1]{2,3,1,0:T(1,128)}, u32[]{:S(2)}, u32[]{:S(2)}) collective-permute-start(f32[6,6,96,1]{2,3,1,0:T(1,128)} %copy.246), channel_id=1, source_target_pairs={{1,0},{2,1},{3,2},{5,4},{6,5},{7,6},{9,8},{10,9},{11,10},{13,12},{... | collective-permute-start | bytes 41480 | tf_op jit(solution)/shard_map/ppermute | solution.py:35
  98.8 16.7 %copy-start.2 = (f32[3,4,96,128]{3,1,2,0:T(4,128)}, f32[3,4,96,128]{3,1,2,0:T(4,128)S(1)}, u32[]{:S(2)}) copy-start(f32[3,4,96,128]{3,1,2,0:T(4,128)S(1)} %slice.698) | copy-start | bytes 1769476
  100.4 8.4 %copy-start.47 = (s32[4,96,128]{2,1,0:T(8,128)S(1)}, s32[4,96,128]{2,1,0:T(8,128)}, u32[]{:S(2)}) copy-start(s32[4,96,128]{2,1,0:T(8,128)} %param.14) | copy-start | bytes 589828
  100.4 8.4 %copy-start.50 = (f32[4,96,128]{2,1,0:T(8,128)S(1)}, f32[4,96,128]{2,1,0:T(8,128)}, u32[]{:S(2)}) copy-start(f32[4,96,128]{2,1,0:T(8,128)} %fusion.96) | copy-start | bytes 589828
  102.5 11.9 %collective-permute-start.8 = (f32[6,1,96,128]{3,1,2,0:T(1,128)S(1)}, f32[6,1,96,128]{3,1,2,0:T(1,128)S(1)}, u32[]{:S(2)}, u32[]{:S(2)}) collective-permute-start(f32[6,1,96,128]{3,1,2,0:T(1,128)S(1)} %get-tuple-element.61), channel_id=1, source_target_pairs={{0,4},{4,8},{8,12},{12,16},{16,20},{20,24},{24,28},{28,32},{32,36}... | collective-permute-start | bytes 884744 | tf_op jit(solution)/shard_map/ppermute | solution.py:33
  106.7 8.8 %collective-permute-start.9 = (f32[6,1,96,128]{3,1,2,0:T(1,128)S(1)}, f32[6,1,96,128]{3,1,2,0:T(1,128)S(1)}, u32[]{:S(2)}, u32[]{:S(2)}) collective-permute-start(f32[6,1,96,128]{3,1,2,0:T(1,128)S(1)} %get-tuple-element.62), channel_id=1, source_target_pairs={{4,0},{8,4},{12,8},{16,12},{20,16},{24,20},{28,24},{32,28},{36,32}... | collective-permute-start | bytes 884744 | tf_op jit(solution)/shard_map/ppermute | solution.py:35
  123.1 11.5 %collective-permute-start.10 = (f32[6,6,96,1]{2,3,1,0:T(1,128)}, f32[6,6,96,1]{2,3,1,0:T(1,128)}, u32[]{:S(2)}, u32[]{:S(2)}) collective-permute-start(f32[6,6,96,1]{2,3,1,0:T(1,128)} %copy.253), channel_id=1, source_target_pairs={{0,1},{1,2},{2,3},{4,5},{5,6},{6,7},{8,9},{9,10},{10,11},{12,13},{... | collective-permute-start | bytes 41480 | tf_op jit(solution)/shard_map/ppermute | solution.py:33
  129.0 7.0 %collective-permute-start.11 = (f32[6,6,96,1]{2,3,1,0:T(1,128)}, f32[6,6,96,1]{2,3,1,0:T(1,128)}, u32[]{:S(2)}, u32[]{:S(2)}) collective-permute-start(f32[6,6,96,1]{2,3,1,0:T(1,128)} %copy.255), channel_id=1, source_target_pairs={{1,0},{2,1},{3,2},{5,4},{6,5},{7,6},{9,8},{10,9},{11,10},{13,12},{... | collective-permute-start | bytes 41480 | tf_op jit(solution)/shard_map/ppermute | solution.py:35
  146.1 20.6 %copy-start = (f32[3,4,96,128]{3,1,2,0:T(4,128)}, f32[3,4,96,128]{3,1,2,0:T(4,128)S(1)}, u32[]{:S(2)}) copy-start(f32[3,4,96,128]{3,1,2,0:T(4,128)S(1)} %slice.722) | copy-start | bytes 1769476
  147.9 9.5 %copy-start.48 = (s32[4,96,128]{2,1,0:T(8,128)S(1)}, s32[4,96,128]{2,1,0:T(8,128)}, u32[]{:S(2)}) copy-start(s32[4,96,128]{2,1,0:T(8,128)} %param.14) | copy-start | bytes 589828
  147.9 9.5 %copy-start.49 = (f32[4,96,128]{2,1,0:T(8,128)S(1)}, f32[4,96,128]{2,1,0:T(8,128)}, u32[]{:S(2)}) copy-start(f32[4,96,128]{2,1,0:T(8,128)} %fusion.93) | copy-start | bytes 589828
  150.4 12.6 %collective-permute-start.12 = (f32[6,1,96,128]{3,1,2,0:T(1,128)S(1)}, f32[6,1,96,128]{3,1,2,0:T(1,128)S(1)}, u32[]{:S(2)}, u32[]{:S(2)}) collective-permute-start(f32[6,1,96,128]{3,1,2,0:T(1,128)S(1)} %get-tuple-element.59), channel_id=1, source_target_pairs={{0,4},{4,8},{8,12},{12,16},{16,20},{20,24},{24,28},{28,32},{32,36}... | collective-permute-start | bytes 884744 | tf_op jit(solution)/shard_map/ppermute | solution.py:33
  155.2 11.5 %collective-permute-start.13 = (f32[6,1,96,128]{3,1,2,0:T(1,128)S(1)}, f32[6,1,96,128]{3,1,2,0:T(1,128)S(1)}, u32[]{:S(2)}, u32[]{:S(2)}) collective-permute-start(f32[6,1,96,128]{3,1,2,0:T(1,128)S(1)} %get-tuple-element.60), channel_id=1, source_target_pairs={{4,0},{8,4},{12,8},{16,12},{20,16},{24,20},{28,24},{32,28},{36,32}... | collective-permute-start | bytes 884744 | tf_op jit(solution)/shard_map/ppermute | solution.py:35
  163.1 3.6 copy-start.31
  174.3 9.5 %collective-permute-start.14 = (f32[6,6,96,1]{2,3,1,0:T(1,128)}, f32[6,6,96,1]{2,3,1,0:T(1,128)}, u32[]{:S(2)}, u32[]{:S(2)}) collective-permute-start(f32[6,6,96,1]{2,3,1,0:T(1,128)} %copy.260), channel_id=1, source_target_pairs={{0,1},{1,2},{2,3},{4,5},{5,6},{6,7},{8,9},{9,10},{10,11},{12,13},{... | collective-permute-start | bytes 41480 | tf_op jit(solution)/shard_map/ppermute | solution.py:33
  178.2 7.1 %collective-permute-start.15 = (f32[6,6,96,1]{2,3,1,0:T(1,128)}, f32[6,6,96,1]{2,3,1,0:T(1,128)}, u32[]{:S(2)}, u32[]{:S(2)}) collective-permute-start(f32[6,6,96,1]{2,3,1,0:T(1,128)} %copy.262), channel_id=1, source_target_pairs={{1,0},{2,1},{3,2},{5,4},{6,5},{7,6},{9,8},{10,9},{11,10},{13,12},{... | collective-permute-start | bytes 41480 | tf_op jit(solution)/shard_map/ppermute | solution.py:35
  196.9 10.6 %copy-start.78 = (f32[64]{0:T(128)S(1)}, f32[64]{0:T(128)}, u32[]{:S(2)}) copy-start(f32[64]{0:T(128)} %add_multiply_fusion.2) | copy-start | bytes 772
  197.0 10.6 %copy-start.79 = (f32[4]{0:T(128)S(1)}, f32[4]{0:T(128)}, u32[]{:S(2)}) copy-start(f32[4]{0:T(128)} %multiply_add_fusion.6) | copy-start | bytes 52
  198.5 16.6 %copy-start.61 = (f32[512]{0:T(512)S(1)}, f32[512]{0:T(512)}, u32[]{:S(2)}) copy-start(f32[512]{0:T(512)} %convert_add_fusion) | copy-start | bytes 6148
  198.5 24.4 %copy-start.60 = (f32[4]{0:T(128)S(1)}, f32[4]{0:T(128)}, u32[]{:S(2)}) copy-start(f32[4]{0:T(128)} %convert_add_fusion.1) | copy-start | bytes 52
  200.0 14.8 %all-to-all-start = ((f32[16,8,4,128]{3,1,2,0:T(8,128)}), f32[16,8,4,128]{3,1,2,0:T(8,128)S(1)}, u32[]{:S(2)}, u32[]{:S(2)}) async-start(f32[16,8,4,128]{3,1,2,0:T(8,128)} %pad_maximum_fusion.44), calls=%async_computation | async-start | bytes 524288 | tf_op jit(solution)/shard_map/all_to_all | solution.py:209
  207.3 346.6 %all-reduce.18.cloned.1.call-start = ((), (), s32[]{:S(2)}) async-start(), calls=%async_computation.1 | async-start | bytes 1048576 | tf_op jit(solution)/shard_map/psum | solution.py:213
  (66 other events, 98.4 us)
Sparse Core Ops, SparseCore 0:
  231.4 322.5 all-reduce.17
where the time goes:
time: 569 us; the launch traced here: 563 us
  waiting for transfers between devices  338 us (59%)
  local copies, waits for them, and re-layouts  71.3 us (13%)
  other arithmetic  70.3 us (12%)
  starting transfers between devices  52.4 us (9%)
  between operations  15.9 us (3%)
  matrix products  14.7 us (3%)
    psum x1, waiting for transfers between devices, local(): lax.psum(contract_x(inner, own_wave, stations, 0, NUX) * scale, 'gx')  322 us
    ppermute x8, starting transfers between devices, extended(): lax.ppermute(tail, axis, [(i, (i + 1) % count) for i in range(ends)])  33.6 us
    slice x8, local copies, waits for them, and re-layouts, extended(): head = lax.slice_in_dim(cells, 0, width, axis=dim)  19.9 us
    add x3, other arithmetic, bloch_update(): inversion + time_step * (recovery * (pump_rate - inversion) - saturation...  17.2 us
    dot_general x8, matrix products, product(): jnp.einsum(form, left, right, precision=lax.Precision.HIGHEST, preferred_...  14.7 us
    squeeze x4, other arithmetic, magnetic_update(): electric_ext[2]  14 us
  transfers between devices with their start and end apart: 18, of which 7 were waited for; matrix products, arithmetic and copies ran while one was open for 8% of the time, Pallas kernels for 0%

commit v1 on v0

v1 whole, which is shorter than its diff:
```python
import functools
import math

import jax
import jax.numpy as jnp
from jax import lax
from jax.experimental import pallas as pl
from jax.experimental.pallas import tpu as pltpu
from jax.sharding import PartitionSpec as P

MESH = pl.DeviceIdType.MESH
F32 = jnp.float32
BF16 = jnp.bfloat16

STEPS = 4
NZ = 96
LX = 4
LANES = 128
CH = 32
NCH = NZ // CH
FL = 4

DT = 0.5
DAMP = 0.4
SAT = 0.5
REC = 0.8
C_DEN = 1.0 + 0.5 * DAMP * DT
C_J = (1.0 - 0.5 * DAMP * DT) / C_DEN
C_D = DT / C_DEN


def sin_turns(turns):
    r = turns - jnp.floor(turns + 0.5)
    x = r * (2.0 * math.pi)
    s = x * x
    acc = jnp.full_like(s, 1.0 / math.factorial(17))
    for order, sign in ((15, -1.0), (13, 1.0), (11, -1.0), (9, 1.0), (7, -1.0), (5, 1.0), (3, -1.0), (1, 1.0)):
        acc = acc * s + sign / math.factorial(order)
    return acc * x


def split(value):
    high = value.astype(BF16)
    return high, (value - high.astype(F32)).astype(BF16)


def dot3(a, b):
    ah, al = a
    bh, bl = b
    dot = functools.partial(jnp.dot, preferred_element_type=F32)
    return dot(ah, bh) + dot(al, bh) + dot(ah, bl)


def kernel(
    e_in, h_in, p_in, j_in, w_in, g_in, r_in, lvl,
    out_e, out_f,
    eb, hb, jb, pb, wb, gb, rb, pump,
    hs, rxe, rxh, rye, ryh, rce, rch, sl, sr,
    gat, tab_h, tab_l, xt_h, xt_l, inn, sbuf, rbuf,
    load_sem, xe_s, xe_r, xh_s, xh_r, l1_s, l2_s, r1_s, r2_s,
    ye_r, yh_r, ce_r, ch_r, g_s, g_r, rs_s, rs_r, out_sem,
):
    gx = lax.axis_index("gx")
    gy = lax.axis_index("gy")
    y_lo = gx // 16
    xc = (gx // 4) % 4
    zc = gx % 4
    left, right = (gx + 31) % 32, (gx + 1) % 32
    down, up = (gy + 3) % 4, (gy + 1) % 4
    has_l, has_r = gx > 0, gx < 31
    has_d, has_u = gy > 0, gy < 3
    dest = y_lo * 4 + zc

    def gather_peers():
        for dx in range(4):
            for dy in range(4):
                if dx or dy:
                    px = y_lo * 16 + ((xc + dx) % 4) * 4 + zc
                    yield (px, (gy + dy) % 4)

    def scatter_peers():
        for d in range(1, 8):
            to = (dest + d) % 8
            yield to, ((to // 4) * 16 + xc * 4 + to % 4, gy)

    loads = [
        pltpu.make_async_copy(e_in, eb.at[0, :, :, pl.ds(0, NZ), :], load_sem.at[0]),
        pltpu.make_async_copy(h_in, hb.at[:, :, pl.ds(8, NZ), :], load_sem.at[1]),
        pltpu.make_async_copy(j_in, jb, load_sem.at[2]),
        pltpu.make_async_copy(p_in, pb, load_sem.at[3]),
        pltpu.make_async_copy(w_in, wb, load_sem.at[4]),
        pltpu.make_async_copy(g_in, gb, load_sem.at[5]),
        pltpu.make_async_copy(r_in, rb, load_sem.at[6]),
    ]
    for copy in loads:
        copy.start()

    barrier = pltpu.get_barrier_semaphore()

    def greet(device):
        pl.semaphore_signal(barrier, inc=1, device_id=device, device_id_type=MESH)

    for peer in gather_peers():
        greet(peer)
    for _, peer in scatter_peers():
        greet(peer)
    pl.when(has_l)(lambda: greet((left, gy)))
    pl.when(has_r)(lambda: greet((right, gy)))
    pl.when(has_l & has_u)(lambda: greet((left, up)))
    pl.when(has_r & has_d)(lambda: greet((right, down)))

    zero_row = jnp.zeros((8, LANES), F32)
    for c in range(3):
        for x in range(LX):
            eb[0, c, x, NZ:, :] = zero_row
            eb[1, c, x, NZ:, :] = zero_row
            hb[c, x, 0:8, :] = zero_row

    @pl.when(jnp.logical_not(has_r))
    def _():
        rxe[...] = jnp.zeros(rxe.shape, F32)

    @pl.when(jnp.logical_not(has_l))
    def _():
        rxh[...] = jnp.zeros(rxh.shape, F32)

    @pl.when(jnp.logical_not(has_u))
    def _():
        rye[...] = jnp.zeros(rye.shape, F32)

    @pl.when(jnp.logical_not(has_d))
    def _():
        ryh[...] = jnp.zeros(ryh.shape, F32)

    @pl.when(jnp.logical_not(has_l & has_u))
    def _():
        rce[...] = jnp.zeros(rce.shape, F32)

    @pl.when(jnp.logical_not(has_r & has_d))
    def _():
        rch[...] = jnp.zeros(rch.shape, F32)

    greeted = (
        22
        + has_l.astype(jnp.int32)
        + has_r.astype(jnp.int32)
        + (has_l & has_u).astype(jnp.int32)
        + (has_r & has_d).astype(jnp.int32)
    )
    pl.semaphore_wait(barrier, greeted)

    keep_l = has_l.astype(F32)
    keep_d = has_d.astype(F32)
    lane = lax.broadcasted_iota(jnp.int32, (CH, LANES), 1)
    first_lane = lane == 0
    last_lane = lane == LANES - 1

    def remote(src, dst, send, recv, device):
        return pltpu.make_async_remote_copy(
            src_ref=src, dst_ref=dst, send_sem=send, recv_sem=recv,
            device_id=device, device_id_type=MESH,
        )

    def xe_copy(s, par):
        return remote(eb.at[par, pl.ds(1, 2), 0, pl.ds(0, NZ), :], rxe.at[s], xe_s.at[s], xe_r.at[s], (left, gy))

    def xh_copy(s):
        return remote(hs.at[s], rxh.at[s], xh_s.at[s], xh_r.at[s], (right, gy))

    def l1_copy(s):
        return remote(sl.at[s], rye.at[s], l1_s.at[s], ye_r.at[s], (gx, down))

    def l2_copy(s):
        return remote(sl.at[s], rce.at[s], l2_s.at[s], ce_r.at[s], (right, down))

    def r1_copy(s):
        return remote(sr.at[s], ryh.at[s], r1_s.at[s], yh_r.at[s], (gx, up))

    def r2_copy(s):
        return remote(sr.at[s], rch.at[s], r2_s.at[s], ch_r.at[s], (left, up))

    def local_h(par, x, cut):
        z = pl.ds(cut * CH, CH)
        z1 = pl.ds(cut * CH + 1, CH)
        zh = pl.ds(8 + cut * CH, CH)
        ex, ey, ez = eb[par, 0, x, z, :], eb[par, 1, x, z, :], eb[par, 2, x, z, :]
        exz, eyz = eb[par, 0, x, z1, :], eb[par, 1, x, z1, :]
        exy = jnp.where(last_lane, 0.0, pltpu.roll(ex, LANES - 1, 1))
        ezy = jnp.where(last_lane, 0.0, pltpu.roll(ez, LANES - 1, 1))
        hx = hb[0, x, zh, :] - DT * ((ezy - ez) - (eyz - ey))
        if x < LX - 1:
            hy = hb[1, x, zh, :] - DT * ((exz - ex) - (eb[par, 2, x + 1, z, :] - ez))
            hz = hb[2, x, zh, :] - DT * ((eb[par, 1, x + 1, z, :] - ey) - (exy - ex))
        else:
            hy = hb[1, x, zh, :] - DT * ((exz - ex) + ez)
            hz = hb[2, x, zh, :] + DT * (ey + (exy - ex))
        return ex, ey, ez, hx, hy, hz

    def put(acc, value, at, to):
        return jnp.where(lane == to, jnp.broadcast_to(value[:, at : at + 1], (CH, LANES)), acc)

    def spread(ref, s, at):
        return jnp.broadcast_to(ref[s, :, at : at + 1], (CH, LANES))

    def e_pass(s, par, x):
        for cut in range(NCH):
            z = pl.ds(cut * CH, CH)
            zh = pl.ds(8 + cut * CH, CH)
            zb = pl.ds(7 + cut * CH, CH)
            ex, ey, ez = eb[par, 0, x, z, :], eb[par, 1, x, z, :], eb[par, 2, x, z, :]
            hx, hy, hz = hb[0, x, zh, :], hb[1, x, zh, :], hb[2, x, zh, :]
            if x == 0:
                hym = keep_l * (rxh[s, 0, z, :] + DT * ez)
                hzm = keep_l * (
                    rxh[s, 1, z, :] - DT * ey
                    + jnp.where(last_lane, DT * spread(rce, s, cut * 16 + 3), 0.0)
                )
            else:
                hym, hzm = hb[1, x - 1, zh, :], hb[2, x - 1, zh, :]
            edge_z = spread(ryh, s, cut * 16 + 4 + x) + DT * ex
            if x == LX - 1:
                edge_z = edge_z - DT * spread(rch, s, cut * 16 + 8)
            edge_x = spread(ryh, s, cut * 16 + x) - DT * ez
            dy_hz = hz - jnp.where(first_lane, keep_d * edge_z, pltpu.roll(hz, 1, 1))
            dy_hx = hx - jnp.where(first_lane, keep_d * edge_x, pltpu.roll(hx, 1, 1))
            curl_x = dy_hz - (hy - hb[1, x, zb, :])
            curl_y = (hx - hb[0, x, zb, :]) - (hz - hzm)
            curl_z = (hy - hym) - dy_hx
            inv = wb[x, z, :]
            gain = gb[x, z, :].astype(F32)
            drop = None
            for c, old, curl in ((0, ex, curl_x), (1, ey, curl_y), (2, ez, curl_z)):
                pol = pb[c, x, z, :]
                cur = gain * (C_J * jb[c, x, z, :] + C_D * (inv * old - pol))
                jb[c, x, z, :] = cur
                pb[c, x, z, :] = pol + DT * cur
                new = old + DT * (curl - cur)
                eb[1 - par, c, x, z, :] = new
                term = (old + new) * cur
                drop = term if drop is None else drop + term
            wb[x, z, :] = (1.0 - DT * REC) * inv + pump[x, z, :] - (0.5 * DT * SAT) * drop

    def wave_turns(col):
        f = gy * FL + col // LANES
        return (0.6 + 0.05 * f.astype(F32)) * (1.0 / (2.0 * math.pi))

    def direction(index):
        return 0.75 * (2.0 * index.astype(F32) - 63.0) / 63.0

    def build_tables():
        rows = 64

        def y_rows(i, carry):
            row = lax.broadcasted_iota(jnp.int32, (rows, LANES), 0) + i * rows
            col = lax.broadcasted_iota(jnp.int32, (rows, LANES), 1)
            base = (row.astype(F32) - 256.0) * direction(col % 64)
            quarter = jnp.where(col < 64, 0.25, 0.0)
            for f in range(FL):
                wave = (0.6 + 0.05 * (gy * FL + f).astype(F32)) * (1.0 / (2.0 * math.pi))
                high, low = split(sin_turns(wave * base + quarter))
                tab_h[pl.ds(i * rows, rows), f * LANES : (f + 1) * LANES] = high
                tab_l[pl.ds(i * rows, rows), f * LANES : (f + 1) * LANES] = low
            return carry

        lax.fori_loop(0, 512 // rows, y_rows, 0)
        row = lax.broadcasted_iota(jnp.int32, (64, LANES), 0)
        col = lax.broadcasted_iota(jnp.int32, (64, LANES), 1)
        to = row // 8
        a = 2 * ((to // 4) * 16 + xc * 4 + to % 4) + (row // 4) % 2
        cell = (y_lo * 16 + ((col % 64) // 16) * 4 + zc) * 4 + col % 4 - 64
        base = cell.astype(F32) * direction(a)
        quarter = jnp.where(col < 64, 0.25, 0.0)
        same = (row % 4) == ((col % 16) // 4)
        for f in range(FL):
            wave = (0.6 + 0.05 * (gy * FL + f).astype(F32)) * (1.0 / (2.0 * math.pi))
            value = jnp.where(same, sin_turns(wave * base + quarter), 0.0) * (1.0 / 256.0)
            high, low = split(value)
            xt_h[f] = high
            xt_l[f] = low
        inn[...] = jnp.zeros(inn.shape, F32)

    gather_bytes = pl.ds(0, 15)

    def gather_copies(n):
        mine = gat.at[n, gy * 4 + xc]
        return [remote(mine, mine, g_s.at[n], g_r.at[n], peer) for peer in gather_peers()]

    def gather_wait(n, sem):
        pltpu.make_async_copy(gat.at[n, gather_bytes], gat.at[n, gather_bytes], sem.at[n]).wait()

    def add_batch(n):
        gather_wait(n, g_r)
        lhs = jnp.concatenate(
            [gat[n, pl.ds(q * 4, 4)].reshape(64, LANES) for q in range(4)], axis=1
        )
        res = dot3(split(lhs), (tab_h[...], tab_l[...]))
        row = lax.broadcasted_iota(jnp.int32, (64, LANES), 0)
        col = lax.broadcasted_iota(jnp.int32, (64, LANES), 1)
        late = jnp.where((row % 16) < 8, 0.5, 1.0) + n.astype(F32)
        sign = jnp.where(col < 64, 1.0, -1.0)
        for f in range(FL):
            wave = (0.6 + 0.05 * (gy * FL + f).astype(F32)) * (1.0 / (2.0 * math.pi))
            turns = wave * DT * late
            part = res[:, f * LANES : (f + 1) * LANES]
            inn[:, f * LANES : (f + 1) * LANES] += DT * (
                sin_turns(turns + 0.25) * part + sin_turns(turns) * (sign * pltpu.roll(part, 64, 1))
            )

    loads[0].wait()
    pl.when(has_l)(lambda: xe_copy(0, 0).start())
    loads[1].wait()

    def step(s, carry):
        par = s % 2
        s = jnp.asarray(s, jnp.int32)
        pack_l = [jnp.zeros((CH, LANES), F32)]
        pack_r = [jnp.zeros((CH, LANES), F32)]

        def pack(cut, x, ex, ey, ez, hx, hz):
            pack_l[0] = put(pack_l[0], ex, 0, cut * 16 + x)
            pack_l[0] = put(pack_l[0], ez, 0, cut * 16 + 4 + x)
            pack_r[0] = put(pack_r[0], hx, LANES - 1, cut * 16 + x)
            pack_r[0] = put(pack_r[0], hz, LANES - 1, cut * 16 + 4 + x)
            if x == 0:
                pack_r[0] = put(pack_r[0], ey, LANES - 1, cut * 16 + 8)

        for x in (3, 0, 1, 2):
            for cut in range(NCH):
                zh = pl.ds(8 + cut * CH, CH)
                ex, ey, ez, hx, hy, hz = local_h(par, x, cut)
                hb[0, x, zh, :] = hx
                hb[1, x, zh, :] = hy
                hb[2, x, zh, :] = hz
                if x == 3:
                    z = pl.ds(cut * CH, CH)
                    hs[s, 0, z, :] = hy
                    hs[s, 1, z, :] = hz
                pack(cut, x, ex, ey, ez, hx, hz)
            if x == 3:
                pl.when(has_r)(lambda: xh_copy(s).start())
        sl[s] = pack_l[0]
        sr[s] = pack_r[0]
        pl.when(has_d)(lambda: l1_copy(s).start())
        pl.when(has_r & has_d)(lambda: l2_copy(s).start())
        pl.when(has_u)(lambda: r1_copy(s).start())
        pl.when(has_l & has_u)(lambda: r2_copy(s).start())

        @pl.when(s == 0)
        def _():
            for copy in loads[2:]:
                copy.wait()
            for x in range(LX):
                for cut in range(NCH):
                    z = pl.ds(cut * CH, CH)
                    region = rb[x, z, :]
                    rate = jnp.zeros((CH, LANES), F32)
                    for k in range(8):
                        rate = jnp.where(region == k, lvl[k], rate)
                    pump[x, z, :] = (DT * REC) * rate
            build_tables()

        @pl.when(s > 0)
        def _():
            add_batch(s - 1)

        pl.when(has_u)(lambda: l1_copy(s).wait_recv())
        pl.when(has_d)(lambda: r1_copy(s).wait_recv())
        pl.when(has_r & has_d)(lambda: r2_copy(s).wait_recv())
        for x in range(LX):
            for cut in range(NCH):
                zh = pl.ds(8 + cut * CH, CH)
                hb[0, x, zh, :] = hb[0, x, zh, :] - jnp.where(last_lane, DT * spread(rye, s, cut * 16 + 4 + x), 0.0)
                hb[2, x, zh, :] = hb[2, x, zh, :] + jnp.where(last_lane, DT * spread(rye, s, cut * 16 + x), 0.0)
        e_pass(s, par, 1)
        e_pass(s, par, 2)

        pl.when(has_l & has_u)(lambda: l2_copy(s).wait_recv())
        pl.when(has_l)(lambda: xh_copy(s).wait_recv())
        e_pass(s, par, 0)

        @pl.when((s < STEPS - 1) & has_l)
        def _():
            xe_copy(s + 1, 1 - par).start()

        pl.when(has_r)(lambda: xe_copy(s, par).wait_recv())
        for cut in range(NCH):
            z = pl.ds(cut * CH, CH)
            zh = pl.ds(8 + cut * CH, CH)
            hb[1, 3, zh, :] = hb[1, 3, zh, :] + DT * rxe[s, 1, z, :]
            hb[2, 3, zh, :] = hb[2, 3, zh, :] - DT * rxe[s, 0, z, :]
        e_pass(s, par, 3)

        me = gy * 4 + xc
        for x in range(LX):
            gat[s, me, pl.ds(x, 1), :] = -hb[1, x, pl.ds(8 + NZ - 1, 1), :]
            gat[s, me, pl.ds(4 + x, 1), :] = hb[0, x, pl.ds(8 + NZ - 1, 1), :]
            gat[s, me, pl.ds(8 + x, 1), :] = eb[1 - par, 1, x, pl.ds(NZ - 1, 1), :]
            gat[s, me, pl.ds(12 + x, 1), :] = -eb[1 - par, 0, x, pl.ds(NZ - 1, 1), :]
        for copy in gather_copies(s):
            copy.start()

        pl.when(has_l)(lambda: xe_copy(s, par).wait_send())
        pl.when(has_r)(lambda: xh_copy(s).wait_send())
        pl.when(has_d)(lambda: l1_copy(s).wait_send())
        pl.when(has_r & has_d)(lambda: l2_copy(s).wait_send())
        pl.when(has_u)(lambda: r1_copy(s).wait_send())
        pl.when(has_l & has_u)(lambda: r2_copy(s).wait_send())
        return carry

    lax.fori_loop(0, STEPS, step, 0)

    final = pltpu.make_async_copy(eb.at[0, :, :, pl.ds(0, NZ), :], out_e, out_sem)
    final.start()
    add_batch(jnp.int32(STEPS - 1))

    col = lax.broadcasted_iota(jnp.int32, (64, LANES), 1)
    sign = jnp.where(col < 64, -1.0, 1.0)
    for f in range(FL):
        part = inn[:, f * LANES : (f + 1) * LANES]
        rhs = jnp.concatenate([part, sign * pltpu.roll(part, 64, 1)], axis=0)
        res = dot3((xt_h[f], xt_l[f]), split(rhs))
        for d in range(8):
            sbuf[d, f] = res[8 * d : 8 * d + 8, :]

    scatter = [
        remote(sbuf.at[to], rbuf.at[dest], rs_s, rs_r, peer) for to, peer in scatter_peers()
    ]
    for copy in scatter:
        copy.start()
    rbuf[dest] = sbuf[dest]
    seven = pl.ds(0, 7)
    pltpu.make_async_copy(rbuf.at[seven], rbuf.at[seven], rs_r).wait()

    low_half = lax.broadcasted_iota(jnp.int32, (1, LANES), 1) < 64
    for f in range(FL):
        total = rbuf[0, f]
        for d in range(1, 8):
            total = total + rbuf[d, f]
        turned = pltpu.roll(total, 64, 1)
        for a in range(2):
            for pair in range(2):
                r0, r1 = a * 4 + 2 * pair, a * 4 + 2 * pair + 1
                real = jnp.where(low_half, total[r0 : r0 + 1, :], turned[r1 : r1 + 1, :])
                imag = jnp.where(low_half, turned[r0 : r0 + 1, :], total[r1 : r1 + 1, :])
                out_f[a, f : f + 1, pair * LANES : (pair + 1) * LANES] = real
                out_f[a, f : f + 1, 256 + pair * LANES : 256 + (pair + 1) * LANES] = imag

    pltpu.make_async_copy(sbuf.at[seven], sbuf.at[seven], rs_s).wait()

    def settle(n, carry):
        gather_wait(n, g_s)
        return carry

    lax.fori_loop(0, STEPS, settle, 0)
    final.wait()


def local(electric, magnetic, polarization, current, inversion, gain_mask, pump_region, pump_level):
    anywhere = pl.BlockSpec(memory_space=pl.ANY)
    dma = pltpu.SemaphoreType.DMA
    vmem = pltpu.VMEM
    state = (3, LX, NZ, LANES)
    return pl.pallas_call(
        kernel,
        out_shape=(
            jax.ShapeDtypeStruct(state, F32),
            jax.ShapeDtypeStruct((2, FL, 512), F32),
        ),
        in_specs=[anywhere] * 7 + [pl.BlockSpec(memory_space=pltpu.SMEM)],
        out_specs=(anywhere, pl.BlockSpec(memory_space=pltpu.VMEM)),
        scratch_shapes=[
            vmem((2, 3, LX, NZ + 8, LANES), F32),
            vmem((3, LX, NZ + 8, LANES), F32),
            vmem(state, F32),
            vmem(state, F32),
            vmem(state[1:], F32),
            vmem(state[1:], jnp.int32),
            vmem(state[1:], jnp.int32),
            vmem(state[1:], F32),
            vmem((STEPS, 2, NZ, LANES), F32),
            vmem((STEPS, 2, NZ, LANES), F32),
            vmem((STEPS, 2, NZ, LANES), F32),
            vmem((STEPS, CH, LANES), F32),
            vmem((STEPS, CH, LANES), F32),
            vmem((STEPS, CH, LANES), F32),
            vmem((STEPS, CH, LANES), F32),
            vmem((STEPS, CH, LANES), F32),
            vmem((STEPS, CH, LANES), F32),
            vmem((STEPS, 16, 16, LANES), F32),
            vmem((512, FL * LANES), BF16),
            vmem((512, FL * LANES), BF16),
            vmem((FL, 64, LANES), BF16),
            vmem((FL, 64, LANES), BF16),
            vmem((64, FL * LANES), F32),
            vmem((8, FL, 8, LANES), F32),
            vmem((8, FL, 8, LANES), F32),
            dma((7,)),
        ]
        + [dma((STEPS,))] * 14
        + [dma, dma, dma],
        compiler_params=pltpu.CompilerParams(
            collective_id=0, has_side_effects=True, vmem_limit_bytes=48 << 20
        ),
    )(electric, magnetic, polarization, current, inversion, gain_mask, pump_region, pump_level)


def solution(mesh):
    return jax.shard_map(
        local,
        mesh=mesh,
        in_specs=(
            P(None, "gx", None, "gy"),
            P(None, "gx", None, "gy"),
            P(None, "gx", None, "gy"),
            P(None, "gx", None, "gy"),
            P("gx", None, "gy"),
            P("gx", None, "gy"),
            P("gx", None, "gy"),
            P(),
        ),
        out_specs=(P(None, "gx", None, "gy"), P("gx", "gy", None)),
        check_vma=False,
    )
```

time: 569 us -> 61.6 us (0.11); the launches traced: 563 us -> 61.3 us
  waiting for transfers between devices: 338 us -> 0 us
  other arithmetic: 70.3 us -> 0 us
  local copies, waits for them, and re-layouts: 71.3 us -> 9.1 us
  starting transfers between devices: 52.4 us -> 0 us
  Pallas kernels: 0 us -> 51.5 us
  between operations: 15.9 us -> 0.66 us
  matrix products: 14.7 us -> 0 us
    psum x1 -> x0, waiting for transfers between devices: 322 us -> none  [local(): lax.psum(contract_x(inner, own_wave, stations, 0, NUX) * scale, 'gx')]
    pallas_call x0 -> x1, Pallas kernels: none -> 51.5 us  [local(): pl.pallas_call(kernel, out_shape=(jax.ShapeDtypeStruct(state, F32), jax.S...]
    ppermute x16 -> x0, starting transfers between devices: 44.9 us -> none  [the longest x8 33.6 us: extended(): lax.ppermute(tail, axis, [(i, (i + 1) % count) for i in range(ends)])]
    slice x33 -> x0, local copies, waits for them, and re-layouts: 28.6 us -> none  [the longest x8 19.9 us: extended(): head = lax.slice_in_dim(cells, 0, width, axis=dim)]
    add x8 -> x0, other arithmetic: 20.6 us -> none  [the longest x3 17.2 us: bloch_update(): inversion + time_step * (recovery * (pump_rate - inversion) - saturation...]
    ppermute x8 -> x0, local copies, waits for them, and re-layouts: 17.1 us -> none  [the longest x4 11.2 us: extended(): lax.ppermute(head, axis, [((i + 1) % count, i) for i in range(ends)])]
    dot_general x8 -> x0, matrix products: 14.7 us -> none  [product(): jnp.einsum(form, left, right, precision=lax.Precision.HIGHEST, preferred_...]
    squeeze x4 -> x0, other arithmetic: 14 us -> none  [magnetic_update(): electric_ext[2]]
  transfers between devices with their start and end apart: 18 -> 0, of which waited for: 7 -> 0; matrix products, arithmetic and copies ran while one was open for 8% -> 0% of each run, Pallas kernels for 0% -> 0%
where the time goes in v1:
time: 61.6 us; the launch traced here: 61.3 us
  Pallas kernels  51.5 us (84%)
  local copies, waits for them, and re-layouts  9.1 us (15%)
  between operations  0.66 us (1%)
    pallas_call x1, Pallas kernels, local(): pl.pallas_call(kernel, out_shape=(jax.ShapeDtypeStruct(state, F32), jax.S...  51.5 us
    unnamed x18, local copies, waits for them, and re-layouts  9.1 us

profile of v1, /device:TPU:0, one launch (start us, length us, event | category | flops | bytes accessed | tf_op | source)
XLA Modules:
  0.0 61.3 jit_solution(16350754406851080681)
XLA Ops:
  0.6 0.0 copy-start
  0.6 1.1 %copy-done = f32[3,4,96,128]{3,2,1,0:T(8,128)S(1)} copy-done((f32[3,4,96,128]{3,2,1,0:T(8,128)S(1)}, f32[3,4,96,128]{3,2,1,0:T(8,128)}, u32[]{:S(2)}) %copy-start) | copy-done | bytes 589848
  1.7 0.0 copy-start.1
  1.7 1.1 %copy-done.1 = f32[3,4,96,128]{3,2,1,0:T(8,128)S(1)} copy-done((f32[3,4,96,128]{3,2,1,0:T(8,128)S(1)}, f32[3,4,96,128]{3,2,1,0:T(8,128)}, u32[]{:S(2)}) %copy-start.1) | copy-done | bytes 589848
  2.8 0.0 copy-start.2
  2.8 1.1 %copy-done.2 = f32[3,4,96,128]{3,2,1,0:T(8,128)S(1)} copy-done((f32[3,4,96,128]{3,2,1,0:T(8,128)S(1)}, f32[3,4,96,128]{3,2,1,0:T(8,128)}, u32[]{:S(2)}) %copy-start.2) | copy-done | bytes 589848
  3.8 0.0 copy-start.3
  3.8 1.1 %copy-done.3 = f32[3,4,96,128]{3,2,1,0:T(8,128)S(1)} copy-done((f32[3,4,96,128]{3,2,1,0:T(8,128)S(1)}, f32[3,4,96,128]{3,2,1,0:T(8,128)}, u32[]{:S(2)}) %copy-start.3) | copy-done | bytes 589848
  4.9 0.0 copy-start.4
  4.9 0.9 %copy-done.4 = f32[4,96,128]{2,1,0:T(8,128)S(1)} copy-done((f32[4,96,128]{2,1,0:T(8,128)S(1)}, f32[4,96,128]{2,1,0:T(8,128)}, u32[]{:S(2)}) %copy-start.4) | copy-done | bytes 196632
  5.8 0.0 copy-start.5
  5.8 0.9 %copy-done.5 = s32[4,96,128]{2,1,0:T(8,128)S(1)} copy-done((s32[4,96,128]{2,1,0:T(8,128)S(1)}, s32[4,96,128]{2,1,0:T(8,128)}, u32[]{:S(2)}) %copy-start.5) | copy-done | bytes 196632
  6.7 0.0 copy-start.6
  6.7 0.9 %copy-done.6 = s32[4,96,128]{2,1,0:T(8,128)S(1)} copy-done((s32[4,96,128]{2,1,0:T(8,128)S(1)}, s32[4,96,128]{2,1,0:T(8,128)}, u32[]{:S(2)}) %copy-start.6) | copy-done | bytes 196632
  7.7 0.0 copy-start.7
  7.7 0.7 %copy-done.7 = f32[8]{0:T(128)S(1)} copy-done((f32[8]{0:T(128)S(1)}, f32[8]{0:T(128)}, u32[]{:S(2)}) %copy-start.7) | copy-done | bytes 56
  8.3 51.5 %shard_map.95 = (f32[3,4,96,128]{3,2,1,0:T(8,128)S(1)}, f32[2,4,512]{2,1,0:T(4,128)S(1)}) custom-call(f32[3,4,96,128]{3,2,1,0:T(8,128)S(1)} %copy-done, f32[3,4,96,128]{3,2,1,0:T(8,128)S(1)} %copy-done.1, f32[3,4,96,128]{3,2,1,0:T(8,128)S(1)} %copy-done.2, f32[3,4,96,128]{3,2,1,0:T(8,128)S(1)} %copy-done.3, f32[4,96,128]{2,1,0:T(8,128)S(1)} %copy-done.4, ...), custom_call_target="tpu_custom_call" | custom-call | tf_op jit(solution)/shard_map/pallas_call | solution.py:463
  59.8 0.8 %copy.12 = f32[3,4,96,128]{3,2,1,0:T(8,128)} copy(f32[3,4,96,128]{3,2,1,0:T(8,128)S(1)} %get-tuple-element.4) | data formatting | bytes 1179648
  60.7 0.6 copy.13
Async XLA Ops:
  0.6 1.1 %copy-start = (f32[3,4,96,128]{3,2,1,0:T(8,128)S(1)}, f32[3,4,96,128]{3,2,1,0:T(8,128)}, u32[]{:S(2)}) copy-start(f32[3,4,96,128]{3,2,1,0:T(8,128)} %e_in.1) | copy-start | bytes 1769476
  1.7 1.1 %copy-start.1 = (f32[3,4,96,128]{3,2,1,0:T(8,128)S(1)}, f32[3,4,96,128]{3,2,1,0:T(8,128)}, u32[]{:S(2)}) copy-start(f32[3,4,96,128]{3,2,1,0:T(8,128)} %h_in.1) | copy-start | bytes 1769476
  2.8 1.1 %copy-start.2 = (f32[3,4,96,128]{3,2,1,0:T(8,128)S(1)}, f32[3,4,96,128]{3,2,1,0:T(8,128)}, u32[]{:S(2)}) copy-start(f32[3,4,96,128]{3,2,1,0:T(8,128)} %p_in.1) | copy-start | bytes 1769476
  3.8 1.1 %copy-start.3 = (f32[3,4,96,128]{3,2,1,0:T(8,128)S(1)}, f32[3,4,96,128]{3,2,1,0:T(8,128)}, u32[]{:S(2)}) copy-start(f32[3,4,96,128]{3,2,1,0:T(8,128)} %j_in.1) | copy-start | bytes 1769476
  4.9 0.9 %copy-start.4 = (f32[4,96,128]{2,1,0:T(8,128)S(1)}, f32[4,96,128]{2,1,0:T(8,128)}, u32[]{:S(2)}) copy-start(f32[4,96,128]{2,1,0:T(8,128)} %w_in.1) | copy-start | bytes 589828
  5.8 0.9 %copy-start.5 = (s32[4,96,128]{2,1,0:T(8,128)S(1)}, s32[4,96,128]{2,1,0:T(8,128)}, u32[]{:S(2)}) copy-start(s32[4,96,128]{2,1,0:T(8,128)} %g_in.1) | copy-start | bytes 589828
  6.7 0.9 %copy-start.6 = (s32[4,96,128]{2,1,0:T(8,128)S(1)}, s32[4,96,128]{2,1,0:T(8,128)}, u32[]{:S(2)}) copy-start(s32[4,96,128]{2,1,0:T(8,128)} %r_in.1) | copy-start | bytes 589828
  7.7 0.7 %copy-start.7 = (f32[8]{0:T(128)S(1)}, f32[8]{0:T(128)}, u32[]{:S(2)}) copy-start(f32[8]{0:T(128)} %lvl.1) | copy-start | bytes 100

commit v2 on v1

--- a/solution.py
+++ b/solution.py
@@ -24,9 +24,8 @@
 DAMP = 0.4
 SAT = 0.5
 REC = 0.8
-C_DEN = 1.0 + 0.5 * DAMP * DT
-C_J = (1.0 - 0.5 * DAMP * DT) / C_DEN
-C_D = DT / C_DEN
+SCALE = DT * DT / (1.0 + 0.5 * DAMP * DT)
+KEEP = (1.0 - 0.5 * DAMP * DT) / (DT * DT)
 
 
 def sin_turns(turns):
@@ -52,12 +51,12 @@
 
 
 def kernel(
-    e_in, h_in, p_in, j_in, w_in, g_in, r_in, lvl,
+    e_in, h_in, p_in, j_in, w_in, g_in, r_in, lvl_in,
     out_e, out_f,
-    eb, hb, jb, pb, wb, gb, rb, pump,
-    hs, rxe, rxh, rye, ryh, rce, rch, sl, sr,
+    eb, hb, jb, pb, wb, gi, gb, rb, pump,
+    hs, rxe, rxh, rye, ryh, rce, rch, sl, sr, tl, tr,
     gat, tab_h, tab_l, xt_h, xt_l, inn, sbuf, rbuf,
-    load_sem, xe_s, xe_r, xh_s, xh_r, l1_s, l2_s, r1_s, r2_s,
+    lvl, load_sem, xe_s, xe_r, xh_s, xh_r, l1_s, l2_s, r1_s, r2_s,
     ye_r, yh_r, ce_r, ch_r, g_s, g_r, rs_s, rs_r, out_sem,
 ):
     gx = lax.axis_index("gx")
@@ -83,14 +82,22 @@
             to = (dest + d) % 8
             yield to, ((to // 4) * 16 + xc * 4 + to % 4, gy)
 
+    def load(src, dst, index):
+        return pltpu.make_async_copy(src, dst, load_sem.at[index])
+
+    body, body_h = pl.ds(0, NZ), pl.ds(8, NZ)
+    inner, outer = pl.ds(0, LX - 1), pl.ds(LX - 1, 1)
     loads = [
-        pltpu.make_async_copy(e_in, eb.at[0, :, :, pl.ds(0, NZ), :], load_sem.at[0]),
-        pltpu.make_async_copy(h_in, hb.at[:, :, pl.ds(8, NZ), :], load_sem.at[1]),
-        pltpu.make_async_copy(j_in, jb, load_sem.at[2]),
-        pltpu.make_async_copy(p_in, pb, load_sem.at[3]),
-        pltpu.make_async_copy(w_in, wb, load_sem.at[4]),
-        pltpu.make_async_copy(g_in, gb, load_sem.at[5]),
-        pltpu.make_async_copy(r_in, rb, load_sem.at[6]),
+        load(e_in.at[:, outer], eb.at[0, :, outer, body, :], 0),
+        load(h_in.at[:, outer], hb.at[:, outer, body_h, :], 1),
+        load(e_in.at[:, inner], eb.at[0, :, inner, body, :], 2),
+        load(h_in.at[:, inner], hb.at[:, inner, body_h, :], 3),
+        load(j_in, jb, 4),
+        load(p_in, pb, 5),
+        load(w_in, wb, 6),
+        load(g_in, gi, 7),
+        load(r_in, rb, 8),
+        load(lvl_in, lvl, 9),
     ]
     for copy in loads:
         copy.start()
@@ -100,14 +107,14 @@
     def greet(device):
         pl.semaphore_signal(barrier, inc=1, device_id=device, device_id_type=MESH)
 
+    pl.when(has_l)(lambda: greet((left, gy)))
+    pl.when(has_r)(lambda: greet((right, gy)))
+    pl.when(has_l & has_u)(lambda: greet((left, up)))
+    pl.when(has_r & has_d)(lambda: greet((right, down)))
     for peer in gather_peers():
         greet(peer)
     for _, peer in scatter_peers():
         greet(peer)
-    pl.when(has_l)(lambda: greet((left, gy)))
-    pl.when(has_r)(lambda: greet((right, gy)))
-    pl.when(has_l & has_u)(lambda: greet((left, up)))
-    pl.when(has_r & has_d)(lambda: greet((right, down)))
 
     zero_row = jnp.zeros((8, LANES), F32)
     for c in range(3):
@@ -115,6 +122,8 @@
             eb[0, c, x, NZ:, :] = zero_row
             eb[1, c, x, NZ:, :] = zero_row
             hb[c, x, 0:8, :] = zero_row
+    for step in range(STEPS):
+        rxe[step, 1, 0:8, :] = zero_row
 
     @pl.when(jnp.logical_not(has_r))
     def _():
@@ -140,17 +149,8 @@
     def _():
         rch[...] = jnp.zeros(rch.shape, F32)
 
-    greeted = (
-        22
-        + has_l.astype(jnp.int32)
-        + has_r.astype(jnp.int32)
-        + (has_l & has_u).astype(jnp.int32)
-        + (has_r & has_d).astype(jnp.int32)
-    )
-    pl.semaphore_wait(barrier, greeted)
-
-    keep_l = has_l.astype(F32)
-    keep_d = has_d.astype(F32)
+    edge_l = has_l.astype(F32) * DT
+    edge_d = has_d.astype(F32) * DT
     lane = lax.broadcasted_iota(jnp.int32, (CH, LANES), 1)
     first_lane = lane == 0
     last_lane = lane == LANES - 1
@@ -161,23 +161,31 @@
             device_id=device, device_id_type=MESH,
         )
 
-    def xe_copy(s, par):
-        return remote(eb.at[par, pl.ds(1, 2), 0, pl.ds(0, NZ), :], rxe.at[s], xe_s.at[s], xe_r.at[s], (left, gy))
-
-    def xh_copy(s):
-        return remote(hs.at[s], rxh.at[s], xh_s.at[s], xh_r.at[s], (right, gy))
+    def xe_copy(s, par, cut):
+        z, zr = pl.ds(cut * CH, CH), pl.ds(8 + cut * CH, CH)
+        return remote(
+            eb.at[par, pl.ds(1, 2), 0, z, :], rxe.at[s, :, zr, :],
+            xe_s.at[s], xe_r.at[s * NCH + cut], (left, gy),
+        )
+
+    def xh_copy(s, cut):
+        z = pl.ds(cut * CH, CH)
+        return remote(
+            hs.at[s, :, z, :], rxh.at[s, :, z, :],
+            xh_s.at[s], xh_r.at[s * NCH + cut], (right, gy),
+        )
 
     def l1_copy(s):
         return remote(sl.at[s], rye.at[s], l1_s.at[s], ye_r.at[s], (gx, down))
 
     def l2_copy(s):
-        return remote(sl.at[s], rce.at[s], l2_s.at[s], ce_r.at[s], (right, down))
+        return remote(tl.at[s], rce.at[s], l2_s.at[s], ce_r.at[s], (right, down))
 
     def r1_copy(s):
         return remote(sr.at[s], ryh.at[s], r1_s.at[s], yh_r.at[s], (gx, up))
 
     def r2_copy(s):
-        return remote(sr.at[s], rch.at[s], r2_s.at[s], ch_r.at[s], (left, up))
+        return remote(tr.at[s], rch.at[s], r2_s.at[s], ch_r.at[s], (left, up))
 
     def local_h(par, x, cut):
         z = pl.ds(cut * CH, CH)
@@ -194,51 +202,108 @@
         else:
             hy = hb[1, x, zh, :] - DT * ((exz - ex) + ez)
             hz = hb[2, x, zh, :] + DT * (ey + (exy - ex))
-        return ex, ey, ez, hx, hy, hz
+        hb[0, x, zh, :] = hx
+        hb[1, x, zh, :] = hy
+        hb[2, x, zh, :] = hz
+        if x == LX - 1:
+            return hy, hz
+        return hx, hz
+
+    def outer_h(s, par, cut):
+        z = pl.ds(cut * CH, CH)
+        hs[s, 0, z, :], hs[s, 1, z, :] = local_h(par, LX - 1, cut)
+
+    def turn(value, at, to):
+        shift = (to - at) % LANES
+        return pltpu.roll(value, shift, 1) if shift else value
 
     def put(acc, value, at, to):
-        return jnp.where(lane == to, jnp.broadcast_to(value[:, at : at + 1], (CH, LANES)), acc)
-
-    def spread(ref, s, at):
-        return jnp.broadcast_to(ref[s, :, at : at + 1], (CH, LANES))
-
-    def e_pass(s, par, x):
+        return jnp.where(lane == to, turn(value, at, to), acc)
+
+    def drop_rate(x, z, drop):
+        wb[x, z, :] = (1.0 - DT * REC) * wb[x, z, :] + pump[x, z, :] - (0.5 * SAT) * drop
+
+    def e_pass(par, x, keep):
         for cut in range(NCH):
             z = pl.ds(cut * CH, CH)
             zh = pl.ds(8 + cut * CH, CH)
             zb = pl.ds(7 + cut * CH, CH)
             ex, ey, ez = eb[par, 0, x, z, :], eb[par, 1, x, z, :], eb[par, 2, x, z, :]
             hx, hy, hz = hb[0, x, zh, :], hb[1, x, zh, :], hb[2, x, zh, :]
+            dy_hz = hz - jnp.where(first_lane, edge_d * ex, pltpu.roll(hz, 1, 1))
+            dy_hx = hx + jnp.where(first_lane, edge_d * ez, -pltpu.roll(hx, 1, 1))
             if x == 0:
-                hym = keep_l * (rxh[s, 0, z, :] + DT * ez)
-                hzm = keep_l * (
-                    rxh[s, 1, z, :] - DT * ey
-                    + jnp.where(last_lane, DT * spread(rce, s, cut * 16 + 3), 0.0)
-                )
+                dx_hz = hz + edge_l * ey
+                dx_hy = hy - edge_l * ez
             else:
-                hym, hzm = hb[1, x - 1, zh, :], hb[2, x - 1, zh, :]
-            edge_z = spread(ryh, s, cut * 16 + 4 + x) + DT * ex
-            if x == LX - 1:
-                edge_z = edge_z - DT * spread(rch, s, cut * 16 + 8)
-            edge_x = spread(ryh, s, cut * 16 + x) - DT * ez
-            dy_hz = hz - jnp.where(first_lane, keep_d * edge_z, pltpu.roll(hz, 1, 1))
-            dy_hx = hx - jnp.where(first_lane, keep_d * edge_x, pltpu.roll(hx, 1, 1))
+                dx_hz = hz - hb[2, x - 1, zh, :]
+                dx_hy = hy - hb[1, x - 1, zh, :]
             curl_x = dy_hz - (hy - hb[1, x, zb, :])
-            curl_y = (hx - hb[0, x, zb, :]) - (hz - hzm)
-            curl_z = (hy - hym) - dy_hx
+            curl_y = (hx - hb[0, x, zb, :]) - dx_hz
+            curl_z = dx_hy - dy_hx
             inv = wb[x, z, :]
-            gain = gb[x, z, :].astype(F32)
-            drop = None
+            gain = gb[x, z, :]
             for c, old, curl in ((0, ex, curl_x), (1, ey, curl_y), (2, ez, curl_z)):
                 pol = pb[c, x, z, :]
-                cur = gain * (C_J * jb[c, x, z, :] + C_D * (inv * old - pol))
+                cur = gain * (keep * jb[c, x, z, :] + (inv * old - pol))
                 jb[c, x, z, :] = cur
-                pb[c, x, z, :] = pol + DT * cur
-                new = old + DT * (curl - cur)
-                eb[1 - par, c, x, z, :] = new
-                term = (old + new) * cur
+                pb[c, x, z, :] = pol + cur
+                eb[1 - par, c, x, z, :] = old + (DT * curl - cur)
+
+    small_lane = lane % 16
+    top_row = lax.broadcasted_iota(jnp.int32, (CH, LANES), 0) == 0
+    edge_lanes = first_lane | last_lane
+
+    def fix_y(s, par):
+        ye, yh = rye[s], ryh[s]
+        ye8, yh8 = pltpu.roll(ye, LANES - 8, 1), pltpu.roll(yh, LANES - 8, 1)
+        under = pltpu.roll(ye8, 1, 0)
+        under = jnp.where(top_row, jnp.where(lane < 16, 0.0, pltpu.roll(under, 16, 1)), under)
+        before = jnp.where(small_lane >= 2, pltpu.roll(ye, 2, 1), 0.0)
+        add_x = (DT * DT) * ye - DT * yh8
+        add_y = (DT * DT) * ((before - ye) - (ye8 - under))
+        add_z = (DT * DT) * ye8 + DT * yh
+        new = 1 - par
+        for x in (0, 3, 1, 2):
+            for cut in range(NCH):
+                z = pl.ds(cut * CH, CH)
+                zh = pl.ds(8 + cut * CH, CH)
+                at = cut * 16 + 2 * x
+                eb[new, 0, x, z, :] = eb[new, 0, x, z, :] + jnp.where(edge_lanes, turn(add_x, at, LANES - 1), 0.0)
+                eb[new, 1, x, z, :] = eb[new, 1, x, z, :] + jnp.where(last_lane, turn(add_y, at, LANES - 1), 0.0)
+                eb[new, 2, x, z, :] = eb[new, 2, x, z, :] + jnp.where(edge_lanes, turn(add_z, at, LANES - 1), 0.0)
+                hb[0, x, zh, :] = hb[0, x, zh, :] - jnp.where(last_lane, DT * turn(ye8, at, LANES - 1), 0.0)
+                hb[2, x, zh, :] = hb[2, x, zh, :] + jnp.where(last_lane, DT * turn(ye, at, LANES - 1), 0.0)
+
+    def late_inversion(par, x):
+        for cut in range(NCH):
+            z = pl.ds(cut * CH, CH)
+            drop = None
+            for c in range(3):
+                term = (eb[par, c, x, z, :] + eb[1 - par, c, x, z, :]) * jb[c, x, z, :]
                 drop = term if drop is None else drop + term
-            wb[x, z, :] = (1.0 - DT * REC) * inv + pump[x, z, :] - (0.5 * DT * SAT) * drop
+            drop_rate(x, z, drop)
+
+    def fix_first(s, par, cut):
+        z = pl.ds(cut * CH, CH)
+        corner = jnp.where(last_lane, (DT * DT) * turn(rce[s], cut * 16, LANES - 1), 0.0)
+        eb[1 - par, 1, 0, z, :] = eb[1 - par, 1, 0, z, :] + (DT * rxh[s, 1, z, :] + corner)
+        eb[1 - par, 2, 0, z, :] = eb[1 - par, 2, 0, z, :] - DT * rxh[s, 0, z, :]
+
+    def fix_outer(s, par, cut):
+        x = LX - 1
+        z = pl.ds(cut * CH, CH)
+        zh = pl.ds(8 + cut * CH, CH)
+        zb = pl.ds(7 + cut * CH, CH)
+        ry = DT * rxe[s, 1, zh, :]
+        rz = DT * rxe[s, 0, zh, :]
+        hb[1, x, zh, :] = hb[1, x, zh, :] + ry
+        hb[2, x, zh, :] = hb[2, x, zh, :] - rz
+        side = jnp.where(first_lane, DT * turn(rch[s], cut * 16, 0), pltpu.roll(rz, 1, 1))
+        back = DT * rxe[s, 1, zb, :]
+        eb[1 - par, 0, x, z, :] = eb[1 - par, 0, x, z, :] + DT * ((side - rz) - (ry - back))
+        eb[1 - par, 1, x, z, :] = eb[1 - par, 1, x, z, :] + DT * rz
+        eb[1 - par, 2, x, z, :] = eb[1 - par, 2, x, z, :] + DT * ry
 
     def wave_turns(col):
         f = gy * FL + col // LANES
@@ -307,47 +372,87 @@
             )
 
     loads[0].wait()
-    pl.when(has_l)(lambda: xe_copy(0, 0).start())
     loads[1].wait()
+    for cut in range(NCH - 1, -1, -1):
+        outer_h(0, 0, cut)
+    loads[2].wait()
+    greeted = (
+        22
+        + has_l.astype(jnp.int32)
+        + has_r.astype(jnp.int32)
+        + (has_l & has_u).astype(jnp.int32)
+        + (has_r & has_d).astype(jnp.int32)
+    )
+    pl.semaphore_wait(barrier, greeted)
+
+    @pl.when(has_l)
+    def _():
+        for cut in range(NCH - 1, -1, -1):
+            xe_copy(0, 0, cut).start()
+
+    @pl.when(has_r)
+    def _():
+        for cut in range(NCH - 1, -1, -1):
+            xh_copy(0, cut).start()
+
+    def send_corners(s, par):
+        left_col = jnp.zeros((CH, LANES), F32)
+        right_col = jnp.zeros((CH, LANES), F32)
+        for cut in range(NCH):
+            z = pl.ds(cut * CH, CH)
+            left_col = put(left_col, eb[par, 0, LX - 1, z, :], 0, cut * 16)
+            right_col = put(right_col, eb[par, 1, 0, z, :], LANES - 1, cut * 16)
+        tl[s] = left_col
+        tr[s] = right_col
+        pl.when(has_r & has_d)(lambda: l2_copy(s).start())
+        pl.when(has_l & has_u)(lambda: r2_copy(s).start())
+
+    def send_low(s, par):
+        pack = jnp.zeros((CH, LANES), F32)
+        for x in range(LX):
+            for cut in range(NCH):
+                z = pl.ds(cut * CH, CH)
+                pack = put(pack, eb[par, 0, x, z, :], 0, cut * 16 + 2 * x)
+                pack = put(pack, eb[par, 2, x, z, :], 0, cut * 16 + 8 + 2 * x)
+        sl[s] = pack
+        pl.when(has_d)(lambda: l1_copy(s).start())
+
+    send_corners(0, 0)
+    loads[3].wait()
+
+    def show_plane(s, par):
+        me = gy * 4 + xc
+        for x in range(LX):
+            gat[s, me, pl.ds(x, 1), :] = -hb[1, x, pl.ds(8 + NZ - 1, 1), :]
+            gat[s, me, pl.ds(4 + x, 1), :] = hb[0, x, pl.ds(8 + NZ - 1, 1), :]
+            gat[s, me, pl.ds(8 + x, 1), :] = eb[1 - par, 1, x, pl.ds(NZ - 1, 1), :]
+            gat[s, me, pl.ds(12 + x, 1), :] = -eb[1 - par, 0, x, pl.ds(NZ - 1, 1), :]
+
+    def gather_start(s):
+        for copy in gather_copies(s):
+            copy.start()
 
     def step(s, carry):
+        s = jnp.asarray(s, jnp.int32)
         par = s % 2
-        s = jnp.asarray(s, jnp.int32)
-        pack_l = [jnp.zeros((CH, LANES), F32)]
-        pack_r = [jnp.zeros((CH, LANES), F32)]
-
-        def pack(cut, x, ex, ey, ez, hx, hz):
-            pack_l[0] = put(pack_l[0], ex, 0, cut * 16 + x)
-            pack_l[0] = put(pack_l[0], ez, 0, cut * 16 + 4 + x)
-            pack_r[0] = put(pack_r[0], hx, LANES - 1, cut * 16 + x)
-            pack_r[0] = put(pack_r[0], hz, LANES - 1, cut * 16 + 4 + x)
-            if x == 0:
-                pack_r[0] = put(pack_r[0], ey, LANES - 1, cut * 16 + 8)
-
+        more = s < STEPS - 1
+        send_low(s, par)
+        pack = jnp.zeros((CH, LANES), F32)
         for x in (3, 0, 1, 2):
             for cut in range(NCH):
-                zh = pl.ds(8 + cut * CH, CH)
-                ex, ey, ez, hx, hy, hz = local_h(par, x, cut)
-                hb[0, x, zh, :] = hx
-                hb[1, x, zh, :] = hy
-                hb[2, x, zh, :] = hz
-                if x == 3:
-                    z = pl.ds(cut * CH, CH)
-                    hs[s, 0, z, :] = hy
-                    hs[s, 1, z, :] = hz
-                pack(cut, x, ex, ey, ez, hx, hz)
-            if x == 3:
-                pl.when(has_r)(lambda: xh_copy(s).start())
-        sl[s] = pack_l[0]
-        sr[s] = pack_r[0]
-        pl.when(has_d)(lambda: l1_copy(s).start())
-        pl.when(has_r & has_d)(lambda: l2_copy(s).start())
+                if x < LX - 1:
+                    hx, hz = local_h(par, x, cut)
+                else:
+                    zh = pl.ds(8 + cut * CH, CH)
+                    hx, hz = hb[0, x, zh, :], hb[2, x, zh, :]
+                pack = put(pack, hx, LANES - 1, cut * 16 + 2 * x + 1)
+                pack = put(pack, hz, LANES - 1, cut * 16 + 8 + 2 * x + 1)
+        sr[s] = pack
         pl.when(has_u)(lambda: r1_copy(s).start())
-        pl.when(has_l & has_u)(lambda: r2_copy(s).start())
 
         @pl.when(s == 0)
         def _():
-            for copy in loads[2:]:
+            for copy in loads[4:]:
                 copy.wait()
             for x in range(LX):
                 for cut in range(NCH):
@@ -357,60 +462,76 @@
                     for k in range(8):
                         rate = jnp.where(region == k, lvl[k], rate)
                     pump[x, z, :] = (DT * REC) * rate
-            build_tables()
+                    gb[x, z, :] = SCALE * gi[x, z, :].astype(F32)
 
         @pl.when(s > 0)
         def _():
-            add_batch(s - 1)
+            for x in range(LX):
+                late_inversion(par, x)
+            gather_start(s - 1)
+
+        keep = jnp.where(s == 0, KEEP * DT, KEEP)
+        for x in (0, 3, 1, 2):
+            e_pass(par, x, keep)
+        pl.when(s == 1)(build_tables)
+        pl.when(s > 1)(lambda: add_batch(s - 2))
 
         pl.when(has_u)(lambda: l1_copy(s).wait_recv())
         pl.when(has_d)(lambda: r1_copy(s).wait_recv())
+        fix_y(s, par)
+
         pl.when(has_r & has_d)(lambda: r2_copy(s).wait_recv())
-        for x in range(LX):
-            for cut in range(NCH):
-                zh = pl.ds(8 + cut * CH, CH)
-                hb[0, x, zh, :] = hb[0, x, zh, :] - jnp.where(last_lane, DT * spread(rye, s, cut * 16 + 4 + x), 0.0)
-                hb[2, x, zh, :] = hb[2, x, zh, :] + jnp.where(last_lane, DT * spread(rye, s, cut * 16 + x), 0.0)
-        e_pass(s, par, 1)
-        e_pass(s, par, 2)
-
         pl.when(has_l & has_u)(lambda: l2_copy(s).wait_recv())
-        pl.when(has_l)(lambda: xh_copy(s).wait_recv())
-        e_pass(s, par, 0)
-
-        @pl.when((s < STEPS - 1) & has_l)
+
+        def finish_outer(cut):
+            fix_outer(s, par, cut)
+
+            @pl.when(more)
+            def _():
+                outer_h(s + 1, 1 - par, cut)
+                pl.when(has_r)(lambda: xh_copy(s + 1, cut).start())
+
+        for cut in range(NCH - 1, -1, -1):
+            pl.when(has_l)(lambda: xh_copy(s, cut).wait_recv())
+            fix_first(s, par, cut)
+            pl.when(more & has_l)(lambda: xe_copy(s + 1, 1 - par, cut).start())
+            pl.when(has_r)(lambda: xe_copy(s, par, cut).wait_recv())
+            if cut < NCH - 1:
+                if cut == NCH - 2:
+                    fix_outer(s, par, cut + 1)
+                    show_plane(s, par)
+
+                    @pl.when(more)
+                    def _():
+                        outer_h(s + 1, 1 - par, cut + 1)
+                        pl.when(has_r)(lambda: xh_copy(s + 1, cut + 1).start())
+
+                    pl.when(jnp.logical_not(more))(lambda: gather_start(s))
+                else:
+                    finish_outer(cut + 1)
+        finish_outer(0)
+        pl.when(more)(lambda: send_corners(s + 1, 1 - par))
+
+        @pl.when(has_l)
         def _():
-            xe_copy(s + 1, 1 - par).start()
-
-        pl.when(has_r)(lambda: xe_copy(s, par).wait_recv())
-        for cut in range(NCH):
-            z = pl.ds(cut * CH, CH)
-            zh = pl.ds(8 + cut * CH, CH)
-            hb[1, 3, zh, :] = hb[1, 3, zh, :] + DT * rxe[s, 1, z, :]
-            hb[2, 3, zh, :] = hb[2, 3, zh, :] - DT * rxe[s, 0, z, :]
-        e_pass(s, par, 3)
-
-        me = gy * 4 + xc
-        for x in range(LX):
-            gat[s, me, pl.ds(x, 1), :] = -hb[1, x, pl.ds(8 + NZ - 1, 1), :]
-            gat[s, me, pl.ds(4 + x, 1), :] = hb[0, x, pl.ds(8 + NZ - 1, 1), :]
-            gat[s, me, pl.ds(8 + x, 1), :] = eb[1 - par, 1, x, pl.ds(NZ - 1, 1), :]
-            gat[s, me, pl.ds(12 + x, 1), :] = -eb[1 - par, 0, x, pl.ds(NZ - 1, 1), :]
-        for copy in gather_copies(s):
-            copy.start()
-
-        pl.when(has_l)(lambda: xe_copy(s, par).wait_send())
-        pl.when(has_r)(lambda: xh_copy(s).wait_send())
+            whole = eb.at[par, pl.ds(1, 2), 0, body, :]
+            remote(whole, rxe.at[s, :, body_h, :], xe_s.at[s], xe_r.at[0], (left, gy)).wait_send()
+
+        @pl.when(has_r)
+        def _():
+            remote(hs.at[s], rxh.at[s], xh_s.at[s], xh_r.at[0], (right, gy)).wait_send()
+
         pl.when(has_d)(lambda: l1_copy(s).wait_send())
+        pl.when(has_u)(lambda: r1_copy(s).wait_send())
         pl.when(has_r & has_d)(lambda: l2_copy(s).wait_send())
-        pl.when(has_u)(lambda: r1_copy(s).wait_send())
         pl.when(has_l & has_u)(lambda: r2_copy(s).wait_send())
         return carry
 
     lax.fori_loop(0, STEPS, step, 0)
 
-    final = pltpu.make_async_copy(eb.at[0, :, :, pl.ds(0, NZ), :], out_e, out_sem)
+    final = pltpu.make_async_copy(eb.at[0, :, :, body, :], out_e, out_sem)
     final.start()
+    add_batch(jnp.int32(STEPS - 2))
     add_batch(jnp.int32(STEPS - 1))
 
     col = lax.broadcasted_iota(jnp.int32, (64, LANES), 1)
@@ -456,18 +577,25 @@
 
 
 def local(electric, magnetic, polarization, current, inversion, gain_mask, pump_region, pump_level):
-    anywhere = pl.BlockSpec(memory_space=pl.ANY)
+    far_memory = pl.BlockSpec(memory_space=pltpu.HBM)
+    near_memory = pl.BlockSpec(memory_space=pltpu.VMEM)
     dma = pltpu.SemaphoreType.DMA
     vmem = pltpu.VMEM
     state = (3, LX, NZ, LANES)
+    operands = [
+        pltpu.with_memory_space_constraint(operand, pltpu.HBM)
+        for operand in (
+            electric, magnetic, polarization, current, inversion, gain_mask, pump_region, pump_level,
+        )
+    ]
     return pl.pallas_call(
         kernel,
         out_shape=(
             jax.ShapeDtypeStruct(state, F32),
             jax.ShapeDtypeStruct((2, FL, 512), F32),
         ),
-        in_specs=[anywhere] * 7 + [pl.BlockSpec(memory_space=pltpu.SMEM)],
-        out_specs=(anywhere, pl.BlockSpec(memory_space=pltpu.VMEM)),
+        in_specs=[far_memory] * 8,
+        out_specs=(near_memory, near_memory),
         scratch_shapes=[
             vmem((2, 3, LX, NZ + 8, LANES), F32),
             vmem((3, LX, NZ + 8, LANES), F32),
@@ -475,11 +603,14 @@
             vmem(state, F32),
             vmem(state[1:], F32),
             vmem(state[1:], jnp.int32),
+            vmem(state[1:], F32),
             vmem(state[1:], jnp.int32),
             vmem(state[1:], F32),
             vmem((STEPS, 2, NZ, LANES), F32),
+            vmem((STEPS, 2, NZ + 8, LANES), F32),
             vmem((STEPS, 2, NZ, LANES), F32),
-            vmem((STEPS, 2, NZ, LANES), F32),
+            vmem((STEPS, CH, LANES), F32),
+            vmem((STEPS, CH, LANES), F32),
             vmem((STEPS, CH, LANES), F32),
             vmem((STEPS, CH, LANES), F32),
             vmem((STEPS, CH, LANES), F32),
@@ -494,14 +625,19 @@
             vmem((64, FL * LANES), F32),
             vmem((8, FL, 8, LANES), F32),
             vmem((8, FL, 8, LANES), F32),
-            dma((7,)),
+            pltpu.SMEM((8,), F32),
+            dma((10,)),
+            dma((STEPS,)),
+            dma((STEPS * NCH,)),
+            dma((STEPS,)),
+            dma((STEPS * NCH,)),
         ]
-        + [dma((STEPS,))] * 14
+        + [dma((STEPS,))] * 10
         + [dma, dma, dma],
         compiler_params=pltpu.CompilerParams(
-            collective_id=0, has_side_effects=True, vmem_limit_bytes=48 << 20
+            collective_id=0, has_side_effects=True, vmem_limit_bytes=24 << 20
         ),
-    )(electric, magnetic, polarization, current, inversion, gain_mask, pump_region, pump_level)
+    )(*operands)
 
 
 def solution(mesh):

time: 61.6 us -> 45.9 us (0.75)
  Pallas kernels: 51.5 us -> 43.5 us
  local copies, waits for them, and re-layouts: 9.1 us -> 1.42 us
    pallas_call x1, Pallas kernels: 51.5 us -> 43.5 us  [local(): pl.pallas_call(kernel, out_shape=(jax.ShapeDtypeStruct(state, F32), jax.S...]
    unnamed x18 -> x2, local copies, waits for them, and re-layouts: 9.1 us -> 1.42 us
where the time goes in v2:
time: 45.9 us; the launch traced here: 45.5 us
  Pallas kernels  43.5 us (95%)
  local copies, waits for them, and re-layouts  1.42 us (3%)
  between operations  0.64 us (1%)
    pallas_call x1, Pallas kernels, local(): pl.pallas_call(kernel, out_shape=(jax.ShapeDtypeStruct(state, F32), jax.S...  43.5 us
    unnamed x2, local copies, waits for them, and re-layouts  1.42 us

profile of v2, /device:TPU:0, one launch (start us, length us, event | category | flops | bytes accessed | tf_op | source)
XLA Modules:
  0.0 45.5 jit_solution(2555145222696444672)
XLA Ops:
  0.6 43.5 %shard_map.95 = (f32[3,4,96,128]{3,2,1,0:T(8,128)S(1)}, f32[2,4,512]{2,1,0:T(4,128)S(1)}) custom-call(f32[3,4,96,128]{3,2,1,0:T(8,128)} %e_in.1, f32[3,4,96,128]{3,2,1,0:T(8,128)} %h_in.1, f32[3,4,96,128]{3,2,1,0:T(8,128)} %p_in.1, f32[3,4,96,128]{3,2,1,0:T(8,128)} %j_in.1, f32[4,96,128]{2,1,0:T(8,128)} %w_in.1, s32[4,96,128]{2,1,0:T(8,128)} %g_in.1, ...), custom_call_target="tpu_custom_call" | custom-call | tf_op jit(solution)/shard_map/pallas_call | solution.py:591
  44.1 0.8 %copy.12 = f32[3,4,96,128]{3,2,1,0:T(8,128)} copy(f32[3,4,96,128]{3,2,1,0:T(8,128)S(1)} %get-tuple-element.4) | data formatting | bytes 1179648
  44.9 0.6 %copy.13 = f32[2,4,512]{2,1,0:T(4,128)} copy(f32[2,4,512]{2,1,0:T(4,128)S(1)} %get-tuple-element.5) | data formatting | bytes 32768

commit v3 on v2

--- a/solution.py
+++ b/solution.py
@@ -55,7 +55,7 @@
     out_e, out_f,
     eb, hb, jb, pb, wb, gi, gb, rb, pump,
     hs, rxe, rxh, rye, ryh, rce, rch, sl, sr, tl, tr,
-    gat, tab_h, tab_l, xt_h, xt_l, inn, sbuf, rbuf,
+    gat, gho, tab_h, tab_l, xt_h, xt_l, inn, sbuf, rbuf,
     lvl, load_sem, xe_s, xe_r, xh_s, xh_r, l1_s, l2_s, r1_s, r2_s,
     ye_r, yh_r, ce_r, ch_r, g_s, g_r, rs_s, rs_r, out_sem,
 ):
@@ -68,19 +68,18 @@
     down, up = (gy + 3) % 4, (gy + 1) % 4
     has_l, has_r = gx > 0, gx < 31
     has_d, has_u = gy > 0, gy < 3
-    dest = y_lo * 4 + zc
+    dest = xc * 4 + zc
 
     def gather_peers():
-        for dx in range(4):
+        for dl in range(2):
             for dy in range(4):
-                if dx or dy:
-                    px = y_lo * 16 + ((xc + dx) % 4) * 4 + zc
-                    yield (px, (gy + dy) % 4)
+                if dl or dy:
+                    yield ((gx + 16 * dl) % 32, (gy + dy) % 4)
 
     def scatter_peers():
-        for d in range(1, 8):
-            to = (dest + d) % 8
-            yield to, ((to // 4) * 16 + xc * 4 + to % 4, gy)
+        for d in range(1, 16):
+            to = (dest + d) % 16
+            yield to, (y_lo * 16 + to, gy)
 
     def load(src, dst, index):
         return pltpu.make_async_copy(src, dst, load_sem.at[index])
@@ -116,6 +115,7 @@
     for _, peer in scatter_peers():
         greet(peer)
 
+    gho[...] = jnp.zeros(gho.shape, F32)
     zero_row = jnp.zeros((8, LANES), F32)
     for c in range(3):
         for x in range(LX):
@@ -151,6 +151,8 @@
 
     edge_l = has_l.astype(F32) * DT
     edge_d = has_d.astype(F32) * DT
+    edge_r = has_r.astype(F32) * DT
+    edge_u = has_u.astype(F32) * DT
     lane = lax.broadcasted_iota(jnp.int32, (CH, LANES), 1)
     first_lane = lane == 0
     last_lane = lane == LANES - 1
@@ -328,26 +330,30 @@
             return carry
 
         lax.fori_loop(0, 512 // rows, y_rows, 0)
-        row = lax.broadcasted_iota(jnp.int32, (64, LANES), 0)
-        col = lax.broadcasted_iota(jnp.int32, (64, LANES), 1)
-        to = row // 8
-        a = 2 * ((to // 4) * 16 + xc * 4 + to % 4) + (row // 4) % 2
-        cell = (y_lo * 16 + ((col % 64) // 16) * 4 + zc) * 4 + col % 4 - 64
+        row = lax.broadcasted_iota(jnp.int32, (128, LANES), 0)
+        col = lax.broadcasted_iota(jnp.int32, (128, LANES), 1)
+        a = 2 * (y_lo * 16 + row // 8) + (row // 4) % 2
+        item = col % 64
+        group = jnp.where(item < 24, 0, 1)
+        r = item - group * 24
+        kind = jnp.where(r < 16, r // 4, jnp.where(r == 17, 0, jnp.where(r == 18, 3, 2)))
+        place = jnp.where(r < 16, r % 4, jnp.where(r == 16, 4, -1))
+        cell = (group * 16 + dest) * 4 + place - 64
         base = cell.astype(F32) * direction(a)
         quarter = jnp.where(col < 64, 0.25, 0.0)
-        same = (row % 4) == ((col % 16) // 4)
+        used = ((row % 4) == kind) & (item < 48) & (r < 20)
         for f in range(FL):
             wave = (0.6 + 0.05 * (gy * FL + f).astype(F32)) * (1.0 / (2.0 * math.pi))
-            value = jnp.where(same, sin_turns(wave * base + quarter), 0.0) * (1.0 / 256.0)
+            value = jnp.where(used, sin_turns(wave * base + quarter), 0.0) * (1.0 / 256.0)
             high, low = split(value)
             xt_h[f] = high
             xt_l[f] = low
         inn[...] = jnp.zeros(inn.shape, F32)
 
-    gather_bytes = pl.ds(0, 15)
+    gather_bytes = pl.ds(0, 7)
 
     def gather_copies(n):
-        mine = gat.at[n, gy * 4 + xc]
+        mine = gat.at[n, gy * 2 + y_lo]
         return [remote(mine, mine, g_s.at[n], g_r.at[n], peer) for peer in gather_peers()]
 
     def gather_wait(n, sem):
@@ -355,21 +361,37 @@
 
     def add_batch(n):
         gather_wait(n, g_r)
-        lhs = jnp.concatenate(
-            [gat[n, pl.ds(q * 4, 4)].reshape(64, LANES) for q in range(4)], axis=1
-        )
+        lane8 = lax.broadcasted_iota(jnp.int32, (8, LANES), 1)
+        first8, last8 = lane8 == 0, lane8 == LANES - 1
+        blocks = []
+        for q in range(4):
+            tiles = []
+            for group in range(2):
+                above = gat[n, (q + 1) * 2 + group, 24:32, :] if q < 3 else None
+                below = gat[n, (q - 1) * 2 + group, 24:32, :] if q > 0 else None
+                for t in range(3):
+                    tile = gat[n, q * 2 + group, 8 * t : 8 * t + 8, :]
+                    if above is not None:
+                        tile = tile + jnp.where(last8, turn(above, 2 * t, 0), 0.0)
+                    if below is not None:
+                        tile = tile + jnp.where(first8, turn(below, 2 * t, 0), 0.0)
+                    tiles.append(tile)
+            blocks.append(jnp.concatenate(tiles, axis=0))
+        lhs = jnp.concatenate(blocks, axis=1)
         res = dot3(split(lhs), (tab_h[...], tab_l[...]))
-        row = lax.broadcasted_iota(jnp.int32, (64, LANES), 0)
-        col = lax.broadcasted_iota(jnp.int32, (64, LANES), 1)
-        late = jnp.where((row % 16) < 8, 0.5, 1.0) + n.astype(F32)
-        sign = jnp.where(col < 64, 1.0, -1.0)
+        row = lax.broadcasted_iota(jnp.int32, (24, LANES), 0)
+        col = lax.broadcasted_iota(jnp.int32, (24, LANES), 1)
+        late = jnp.where((row < 8) | (row == 17), 0.5, 1.0) + n.astype(F32)
+        sign = jnp.where(col < 64, DT, -DT)
         for f in range(FL):
             wave = (0.6 + 0.05 * (gy * FL + f).astype(F32)) * (1.0 / (2.0 * math.pi))
             turns = wave * DT * late
-            part = res[:, f * LANES : (f + 1) * LANES]
-            inn[:, f * LANES : (f + 1) * LANES] += DT * (
-                sin_turns(turns + 0.25) * part + sin_turns(turns) * (sign * pltpu.roll(part, 64, 1))
-            )
+            real = DT * sin_turns(turns + 0.25)
+            imag = sign * sin_turns(turns)
+            for group in range(2):
+                part = res[group * 24 : (group + 1) * 24, f * LANES : (f + 1) * LANES]
+                rows = pl.ds(group * 24, 24)
+                inn[rows, f * LANES : (f + 1) * LANES] += real * part + imag * pltpu.roll(part, 64, 1)
 
     loads[0].wait()
     loads[1].wait()
@@ -407,26 +429,90 @@
         pl.when(has_r & has_d)(lambda: l2_copy(s).start())
         pl.when(has_l & has_u)(lambda: r2_copy(s).start())
 
-    def send_low(s, par):
-        pack = jnp.zeros((CH, LANES), F32)
-        for x in range(LX):
-            for cut in range(NCH):
-                z = pl.ds(cut * CH, CH)
-                pack = put(pack, eb[par, 0, x, z, :], 0, cut * 16 + 2 * x)
-                pack = put(pack, eb[par, 2, x, z, :], 0, cut * 16 + 8 + 2 * x)
-        sl[s] = pack
+    def put_low(pack, par, x):
+        for cut in range(NCH):
+            z = pl.ds(cut * CH, CH)
+            pack = put(pack, eb[par, 0, x, z, :], 0, cut * 16 + 2 * x)
+            pack = put(pack, eb[par, 2, x, z, :], 0, cut * 16 + 8 + 2 * x)
+        return pack
+
+    def put_high(pack, par, x):
+        for cut in range(NCH):
+            if x < LX - 1:
+                hx, hz = local_h(par, x, cut)
+            else:
+                zh = pl.ds(8 + cut * CH, CH)
+                hx, hz = hb[0, x, zh, :], hb[2, x, zh, :]
+            pack = put(pack, hx, LANES - 1, cut * 16 + 2 * x + 1)
+            pack = put(pack, hz, LANES - 1, cut * 16 + 8 + 2 * x + 1)
+        return pack
+
+    def early_pack(s, par):
+        none = jnp.zeros((CH, LANES), F32)
+        sl[s] = put_low(put_low(none, par, 1), par, 2)
+        sr[s] = put_high(none, par, 1)
+
+    def late_pack(s, par):
+        sl[s] = put_low(put_low(sl[s], par, 0), par, 3)
         pl.when(has_d)(lambda: l1_copy(s).start())
+        sr[s] = put_high(put_high(put_high(sr[s], par, 3), par, 0), par, 2)
+        pl.when(has_u)(lambda: r1_copy(s).start())
 
     send_corners(0, 0)
     loads[3].wait()
-
-    def show_plane(s, par):
-        me = gy * 4 + xc
+    early_pack(0, 0)
+
+    def far_slab(s, par, keep):
+        me = gy * 2 + y_lo
+        z, zl, zh, zb = pl.ds(NZ - 8, 8), pl.ds(NZ - 9, 8), pl.ds(NZ, 8), pl.ds(NZ - 1, 8)
+        lane8 = lax.broadcasted_iota(jnp.int32, (8, LANES), 1)
+        first8, last8 = lane8 == 0, lane8 == LANES - 1
+        nothing = jnp.zeros((8, LANES), F32)
+
+        def show(row, value):
+            gat[s, me, row : row + 1, :] = value[7:8, :]
+
+        def ghost(row, low, high):
+            value = nothing
+            if low is not None:
+                value = jnp.where(last8, pltpu.roll(low, LANES - 1, 1), value)
+            if high is not None:
+                value = jnp.where(first8, pltpu.roll(high, 1, 1), value)
+            gho[row : row + 1, :] = value[7:8, :]
+
+        gat[s, me, 16:24, :] = nothing
         for x in range(LX):
-            gat[s, me, pl.ds(x, 1), :] = -hb[1, x, pl.ds(8 + NZ - 1, 1), :]
-            gat[s, me, pl.ds(4 + x, 1), :] = hb[0, x, pl.ds(8 + NZ - 1, 1), :]
-            gat[s, me, pl.ds(8 + x, 1), :] = eb[1 - par, 1, x, pl.ds(NZ - 1, 1), :]
-            gat[s, me, pl.ds(12 + x, 1), :] = -eb[1 - par, 0, x, pl.ds(NZ - 1, 1), :]
+            ex, ey, ez = eb[par, 0, x, z, :], eb[par, 1, x, z, :], eb[par, 2, x, z, :]
+            hx, hy, hz = hb[0, x, zh, :], hb[1, x, zh, :], hb[2, x, zh, :]
+            dy_hz = hz - jnp.where(first8, edge_d * ex, pltpu.roll(hz, 1, 1))
+            dx_hz = hz + edge_l * ey if x == 0 else hz - hb[2, x - 1, zh, :]
+            curl_x = dy_hz - (hy - hb[1, x, zb, :])
+            curl_y = (hx - hb[0, x, zb, :]) - dx_hz
+            inv, gain = wb[x, z, :], gb[x, z, :]
+            cur_x = gain * (keep * jb[0, x, z, :] + (inv * ex - pb[0, x, z, :]))
+            cur_y = gain * (keep * jb[1, x, z, :] + (inv * ey - pb[1, x, z, :]))
+            show(x, -hy)
+            show(4 + x, hx)
+            show(8 + x, ey + (DT * curl_y - cur_y))
+            show(12 + x, -(ex + (DT * curl_x - cur_x)))
+            rise = ez - eb[par, 2, x, zl, :]
+            side = -rise - ex if x == 0 else eb[par, 0, x - 1, z, :] - rise - ex
+            ghost(4 + x, -edge_d * ez, None)
+            ghost(8 + x, (DT * edge_d) * side, None)
+            ghost(12 + x, -(DT * edge_d) * ex, edge_u * hz)
+            if x == LX - 1:
+                show(16, edge_r * hz)
+                ghost(16, (edge_r * edge_d) * ex, None)
+            if x == 0:
+                rz = edge_l * ey
+                before = jnp.where(first8, 0.0, pltpu.roll(rz, 1, 1))
+                show(17, -edge_l * ez)
+                show(18, DT * ((rz - before) + edge_l * rise))
+                show(19, DT * rz)
+                ghost(18, None, -edge_u * rz)
+        gat[s, me, 24:32, :] = (
+            gho[0:8, :] + pltpu.roll(gho[8:16, :], 2, 1) + pltpu.roll(gho[16:24, :], 4, 1)
+        )
 
     def gather_start(s):
         for copy in gather_copies(s):
@@ -436,19 +522,7 @@
         s = jnp.asarray(s, jnp.int32)
         par = s % 2
         more = s < STEPS - 1
-        send_low(s, par)
-        pack = jnp.zeros((CH, LANES), F32)
-        for x in (3, 0, 1, 2):
-            for cut in range(NCH):
-                if x < LX - 1:
-                    hx, hz = local_h(par, x, cut)
-                else:
-                    zh = pl.ds(8 + cut * CH, CH)
-                    hx, hz = hb[0, x, zh, :], hb[2, x, zh, :]
-                pack = put(pack, hx, LANES - 1, cut * 16 + 2 * x + 1)
-                pack = put(pack, hz, LANES - 1, cut * 16 + 8 + 2 * x + 1)
-        sr[s] = pack
-        pl.when(has_u)(lambda: r1_copy(s).start())
+        late_pack(s, par)
 
         @pl.when(s == 0)
         def _():
@@ -468,24 +542,28 @@
         def _():
             for x in range(LX):
                 late_inversion(par, x)
-            gather_start(s - 1)
 
         keep = jnp.where(s == 0, KEEP * DT, KEEP)
+        far_slab(s, par, keep)
+        gather_start(s)
         for x in (0, 3, 1, 2):
             e_pass(par, x, keep)
-        pl.when(s == 1)(build_tables)
-        pl.when(s > 1)(lambda: add_batch(s - 2))
+        pl.when(s == 0)(build_tables)
+        pl.when(s > 0)(lambda: add_batch(s - 1))
 
         pl.when(has_u)(lambda: l1_copy(s).wait_recv())
         pl.when(has_d)(lambda: r1_copy(s).wait_recv())
         fix_y(s, par)
 
+        pl.when(more)(lambda: early_pack(s + 1, 1 - par))
+
         pl.when(has_r & has_d)(lambda: r2_copy(s).wait_recv())
         pl.when(has_l & has_u)(lambda: l2_copy(s).wait_recv())
 
-        def finish_outer(cut):
-            fix_outer(s, par, cut)
-
+        def next_low(cut):
+            pl.when(more & has_l)(lambda: xe_copy(s + 1, 1 - par, cut).start())
+
+        def next_high(cut):
             @pl.when(more)
             def _():
                 outer_h(s + 1, 1 - par, cut)
@@ -494,23 +572,18 @@
         for cut in range(NCH - 1, -1, -1):
             pl.when(has_l)(lambda: xh_copy(s, cut).wait_recv())
             fix_first(s, par, cut)
-            pl.when(more & has_l)(lambda: xe_copy(s + 1, 1 - par, cut).start())
+            if cut > 0:
+                next_low(cut)
             pl.when(has_r)(lambda: xe_copy(s, par, cut).wait_recv())
             if cut < NCH - 1:
-                if cut == NCH - 2:
-                    fix_outer(s, par, cut + 1)
-                    show_plane(s, par)
-
-                    @pl.when(more)
-                    def _():
-                        outer_h(s + 1, 1 - par, cut + 1)
-                        pl.when(has_r)(lambda: xh_copy(s + 1, cut + 1).start())
-
-                    pl.when(jnp.logical_not(more))(lambda: gather_start(s))
-                else:
-                    finish_outer(cut + 1)
-        finish_outer(0)
+                fix_outer(s, par, cut + 1)
+            if 0 < cut < NCH - 1:
+                next_high(cut + 1)
+        fix_outer(s, par, 0)
         pl.when(more)(lambda: send_corners(s + 1, 1 - par))
+        next_low(0)
+        next_high(1)
+        next_high(0)
 
         @pl.when(has_l)
         def _():
@@ -531,16 +604,16 @@
 
     final = pltpu.make_async_copy(eb.at[0, :, :, body, :], out_e, out_sem)
     final.start()
-    add_batch(jnp.int32(STEPS - 2))
     add_batch(jnp.int32(STEPS - 1))
 
-    col = lax.broadcasted_iota(jnp.int32, (64, LANES), 1)
+    col = lax.broadcasted_iota(jnp.int32, (48, LANES), 1)
     sign = jnp.where(col < 64, -1.0, 1.0)
+    filler = jnp.zeros((16, LANES), F32)
     for f in range(FL):
         part = inn[:, f * LANES : (f + 1) * LANES]
-        rhs = jnp.concatenate([part, sign * pltpu.roll(part, 64, 1)], axis=0)
+        rhs = jnp.concatenate([part, filler, sign * pltpu.roll(part, 64, 1), filler], axis=0)
         res = dot3((xt_h[f], xt_l[f]), split(rhs))
-        for d in range(8):
+        for d in range(16):
             sbuf[d, f] = res[8 * d : 8 * d + 8, :]
 
     scatter = [
@@ -549,13 +622,13 @@
     for copy in scatter:
         copy.start()
     rbuf[dest] = sbuf[dest]
-    seven = pl.ds(0, 7)
-    pltpu.make_async_copy(rbuf.at[seven], rbuf.at[seven], rs_r).wait()
+    fifteen = pl.ds(0, 15)
+    pltpu.make_async_copy(rbuf.at[fifteen], rbuf.at[fifteen], rs_r).wait()
 
     low_half = lax.broadcasted_iota(jnp.int32, (1, LANES), 1) < 64
     for f in range(FL):
         total = rbuf[0, f]
-        for d in range(1, 8):
+        for d in range(1, 16):
             total = total + rbuf[d, f]
         turned = pltpu.roll(total, 64, 1)
         for a in range(2):
@@ -566,7 +639,7 @@
                 out_f[a, f : f + 1, pair * LANES : (pair + 1) * LANES] = real
                 out_f[a, f : f + 1, 256 + pair * LANES : 256 + (pair + 1) * LANES] = imag
 
-    pltpu.make_async_copy(sbuf.at[seven], sbuf.at[seven], rs_s).wait()
+    pltpu.make_async_copy(sbuf.at[fifteen], sbuf.at[fifteen], rs_s).wait()
 
     def settle(n, carry):
         gather_wait(n, g_s)
@@ -617,14 +690,15 @@
             vmem((STEPS, CH, LANES), F32),
             vmem((STEPS, CH, LANES), F32),
             vmem((STEPS, CH, LANES), F32),
-            vmem((STEPS, 16, 16, LANES), F32),
+            vmem((STEPS, 8, 32, LANES), F32),
+            vmem((24, LANES), F32),
             vmem((512, FL * LANES), BF16),
             vmem((512, FL * LANES), BF16),
-            vmem((FL, 64, LANES), BF16),
-            vmem((FL, 64, LANES), BF16),
-            vmem((64, FL * LANES), F32),
-            vmem((8, FL, 8, LANES), F32),
-            vmem((8, FL, 8, LANES), F32),
+            vmem((FL, 128, LANES), BF16),
+            vmem((FL, 128, LANES), BF16),
+            vmem((48, FL * LANES), F32),
+            vmem((16, FL, 8, LANES), F32),
+            vmem((16, FL, 8, LANES), F32),
             pltpu.SMEM((8,), F32),
             dma((10,)),
             dma((STEPS,)),

time: 45.9 us -> 41.4 us (0.902)
  Pallas kernels: 43.5 us -> 39.2 us
    pallas_call x1, Pallas kernels: 43.5 us -> 39.2 us  [local(): pl.pallas_call(kernel, out_shape=(jax.ShapeDtypeStruct(state, F32), jax.S...]
where the time goes in v3:
time: 41.4 us; the launch traced here: 41.2 us
  Pallas kernels  39.2 us (95%)
  local copies, waits for them, and re-layouts  1.42 us (3%)
  between operations  0.64 us (2%)
    pallas_call x1, Pallas kernels, local(): pl.pallas_call(kernel, out_shape=(jax.ShapeDtypeStruct(state, F32), jax.S...  39.2 us
    unnamed x2, local copies, waits for them, and re-layouts  1.42 us

profile of v3, /device:TPU:0, one launch (start us, length us, event | category | flops | bytes accessed | tf_op | source)
XLA Modules:
  0.0 41.2 jit_solution(9009018458405652479)
XLA Ops:
  0.6 39.2 %shard_map.95 = (f32[3,4,96,128]{3,2,1,0:T(8,128)S(1)}, f32[2,4,512]{2,1,0:T(4,128)S(1)}) custom-call(f32[3,4,96,128]{3,2,1,0:T(8,128)} %e_in.1, f32[3,4,96,128]{3,2,1,0:T(8,128)} %h_in.1, f32[3,4,96,128]{3,2,1,0:T(8,128)} %p_in.1, f32[3,4,96,128]{3,2,1,0:T(8,128)} %j_in.1, f32[4,96,128]{2,1,0:T(8,128)} %w_in.1, s32[4,96,128]{2,1,0:T(8,128)} %g_in.1, ...), custom_call_target="tpu_custom_call" | custom-call | tf_op jit(solution)/shard_map/pallas_call | solution.py:664
  39.8 0.8 %copy.12 = f32[3,4,96,128]{3,2,1,0:T(8,128)} copy(f32[3,4,96,128]{3,2,1,0:T(8,128)S(1)} %get-tuple-element.4) | data formatting | bytes 1179648
  40.6 0.6 %copy.13 = f32[2,4,512]{2,1,0:T(4,128)} copy(f32[2,4,512]{2,1,0:T(4,128)S(1)} %get-tuple-element.5) | data formatting | bytes 32768

commit v4 on v3

--- a/solution.py
+++ b/solution.py
@@ -277,8 +277,8 @@
                 hb[0, x, zh, :] = hb[0, x, zh, :] - jnp.where(last_lane, DT * turn(ye8, at, LANES - 1), 0.0)
                 hb[2, x, zh, :] = hb[2, x, zh, :] + jnp.where(last_lane, DT * turn(ye, at, LANES - 1), 0.0)
 
-    def late_inversion(par, x):
-        for cut in range(NCH):
+    def late_inversion(par, x, cuts):
+        for cut in cuts:
             z = pl.ds(cut * CH, CH)
             drop = None
             for c in range(3):
@@ -436,9 +436,9 @@
             pack = put(pack, eb[par, 2, x, z, :], 0, cut * 16 + 8 + 2 * x)
         return pack
 
-    def put_high(pack, par, x):
+    def put_high(pack, par, x, done=False):
         for cut in range(NCH):
-            if x < LX - 1:
+            if x < LX - 1 and not done:
                 hx, hz = local_h(par, x, cut)
             else:
                 zh = pl.ds(8 + cut * CH, CH)
@@ -452,10 +452,10 @@
         sl[s] = put_low(put_low(none, par, 1), par, 2)
         sr[s] = put_high(none, par, 1)
 
-    def late_pack(s, par):
+    def late_pack(s, par, done=False):
         sl[s] = put_low(put_low(sl[s], par, 0), par, 3)
         pl.when(has_d)(lambda: l1_copy(s).start())
-        sr[s] = put_high(put_high(put_high(sr[s], par, 3), par, 0), par, 2)
+        sr[s] = put_high(put_high(put_high(sr[s], par, 3), par, 0, done), par, 2, done)
         pl.when(has_u)(lambda: r1_copy(s).start())
 
     send_corners(0, 0)
@@ -518,11 +518,13 @@
         for copy in gather_copies(s):
             copy.start()
 
-    def step(s, carry):
-        s = jnp.asarray(s, jnp.int32)
-        par = s % 2
-        more = s < STEPS - 1
-        late_pack(s, par)
+    def first_half(s, par, last):
+        if last:
+            for x in (0, 2):
+                for cut in range(NCH):
+                    local_h(par, x, cut)
+        else:
+            late_pack(s, par)
 
         @pl.when(s == 0)
         def _():
@@ -538,34 +540,44 @@
                     pump[x, z, :] = (DT * REC) * rate
                     gb[x, z, :] = SCALE * gi[x, z, :].astype(F32)
 
-        @pl.when(s > 0)
-        def _():
-            for x in range(LX):
-                late_inversion(par, x)
+        def invert(cuts):
+            @pl.when(s > 0)
+            def _():
+                for x in range(LX):
+                    late_inversion(par, x, cuts)
 
         keep = jnp.where(s == 0, KEEP * DT, KEEP)
+        invert((NCH - 1,))
         far_slab(s, par, keep)
         gather_start(s)
+        if last:
+            late_pack(s, par, True)
+        invert(range(NCH - 1))
         for x in (0, 3, 1, 2):
             e_pass(par, x, keep)
         pl.when(s == 0)(build_tables)
-        pl.when(s > 0)(lambda: add_batch(s - 1))
-
+        pl.when(s > 0)(lambda: add_batch(jnp.asarray(s - 1, jnp.int32)))
+
+
+    def y_half(s, par):
         pl.when(has_u)(lambda: l1_copy(s).wait_recv())
         pl.when(has_d)(lambda: r1_copy(s).wait_recv())
         fix_y(s, par)
 
-        pl.when(more)(lambda: early_pack(s + 1, 1 - par))
+
+    def second_half(s, par, more):
+        if more:
+            early_pack(s + 1, 1 - par)
 
         pl.when(has_r & has_d)(lambda: r2_copy(s).wait_recv())
         pl.when(has_l & has_u)(lambda: l2_copy(s).wait_recv())
 
         def next_low(cut):
-            pl.when(more & has_l)(lambda: xe_copy(s + 1, 1 - par, cut).start())
+            if more:
+                pl.when(has_l)(lambda: xe_copy(s + 1, 1 - par, cut).start())
 
         def next_high(cut):
-            @pl.when(more)
-            def _():
+            if more:
                 outer_h(s + 1, 1 - par, cut)
                 pl.when(has_r)(lambda: xh_copy(s + 1, cut).start())
 
@@ -580,7 +592,8 @@
             if 0 < cut < NCH - 1:
                 next_high(cut + 1)
         fix_outer(s, par, 0)
-        pl.when(more)(lambda: send_corners(s + 1, 1 - par))
+        if more:
+            send_corners(s + 1, 1 - par)
         next_low(0)
         next_high(1)
         next_high(0)
@@ -598,12 +611,16 @@
         pl.when(has_u)(lambda: r1_copy(s).wait_send())
         pl.when(has_r & has_d)(lambda: l2_copy(s).wait_send())
         pl.when(has_l & has_u)(lambda: r2_copy(s).wait_send())
+    def step(s, carry):
+        s = jnp.asarray(s, jnp.int32)
+        first_half(s, s % 2, False)
+        y_half(s, s % 2)
+        second_half(s, s % 2, True)
         return carry
 
-    lax.fori_loop(0, STEPS, step, 0)
-
-    final = pltpu.make_async_copy(eb.at[0, :, :, body, :], out_e, out_sem)
-    final.start()
+    lax.fori_loop(0, STEPS - 1, step, 0)
+
+    first_half(STEPS - 1, 1, True)
     add_batch(jnp.int32(STEPS - 1))
 
     col = lax.broadcasted_iota(jnp.int32, (48, LANES), 1)
@@ -622,6 +639,12 @@
     for copy in scatter:
         copy.start()
     rbuf[dest] = sbuf[dest]
+
+    y_half(STEPS - 1, 1)
+    second_half(STEPS - 1, 1, False)
+    final = pltpu.make_async_copy(eb.at[0, :, :, body, :], out_e, out_sem)
+    final.start()
+
     fifteen = pl.ds(0, 15)
     pltpu.make_async_copy(rbuf.at[fifteen], rbuf.at[fifteen], rs_r).wait()
 
@@ -649,7 +672,19 @@
     final.wait()
 
 
+def store(field, far, out_e, out_f, field_sem, far_sem):
+    copies = [
+        pltpu.make_async_copy(far, out_f, far_sem),
+        pltpu.make_async_copy(field, out_e, field_sem),
+    ]
+    for copy in copies:
+        copy.start()
+    for copy in copies:
+        copy.wait()
+
+
 def local(electric, magnetic, polarization, current, inversion, gain_mask, pump_region, pump_level):
+    anywhere = pl.BlockSpec(memory_space=pl.ANY)
     far_memory = pl.BlockSpec(memory_space=pltpu.HBM)
     near_memory = pl.BlockSpec(memory_space=pltpu.VMEM)
     dma = pltpu.SemaphoreType.DMA
@@ -661,7 +696,7 @@
             electric, magnetic, polarization, current, inversion, gain_mask, pump_region, pump_level,
         )
     ]
-    return pl.pallas_call(
+    field, far = pl.pallas_call(
         kernel,
         out_shape=(
             jax.ShapeDtypeStruct(state, F32),
@@ -712,6 +747,17 @@
             collective_id=0, has_side_effects=True, vmem_limit_bytes=24 << 20
         ),
     )(*operands)
+    return pl.pallas_call(
+        store,
+        out_shape=(
+            jax.ShapeDtypeStruct(state, F32),
+            jax.ShapeDtypeStruct((2, FL, 512), F32),
+        ),
+        in_specs=[anywhere] * 2,
+        out_specs=(anywhere, anywhere),
+        scratch_shapes=[dma, dma],
+        compiler_params=pltpu.CompilerParams(vmem_limit_bytes=1 << 20),
+    )(field, far)
 
 
 def solution(mesh):

time: 41.4 us -> 39.6 us (0.957)
  local copies, waits for them, and re-layouts: 1.42 us -> 0 us
    unnamed x2 -> x0, local copies, waits for them, and re-layouts: 1.42 us -> none
    pallas_call x1, Pallas kernels: 39.2 us -> 38 us  [local(): pl.pallas_call(kernel, out_shape=(jax.ShapeDtypeStruct(state, F32), jax.S...]
    pallas_call x0 -> x1, Pallas kernels: none -> 0.84 us  [local(): pl.pallas_call(store, out_shape=(jax.ShapeDtypeStruct(state, F32), jax.Sh...]
where the time goes in v4:
time: 39.6 us; the launch traced here: 39.4 us
  Pallas kernels  38.8 us (98%)
  between operations  0.64 us (2%)
    pallas_call x1, Pallas kernels, local(): pl.pallas_call(kernel, out_shape=(jax.ShapeDtypeStruct(state, F32), jax.S...  38 us
    pallas_call x1, Pallas kernels, local(): pl.pallas_call(store, out_shape=(jax.ShapeDtypeStruct(state, F32), jax.Sh...  0.84 us

profile of v4, /device:TPU:0, one launch (start us, length us, event | category | flops | bytes accessed | tf_op | source)
XLA Modules:
  0.0 39.4 jit_solution(4237747733664942711)
XLA Ops:
  0.6 38.0 %shard_map.95 = (f32[3,4,96,128]{3,2,1,0:T(8,128)S(1)}, f32[2,4,512]{2,1,0:T(4,128)S(1)}) custom-call(f32[3,4,96,128]{3,2,1,0:T(8,128)} %e_in.1, f32[3,4,96,128]{3,2,1,0:T(8,128)} %h_in.1, f32[3,4,96,128]{3,2,1,0:T(8,128)} %p_in.1, f32[3,4,96,128]{3,2,1,0:T(8,128)} %j_in.1, f32[4,96,128]{2,1,0:T(8,128)} %w_in.1, s32[4,96,128]{2,1,0:T(8,128)} %g_in.1, ...), custom_call_target="tpu_custom_call" | custom-call | tf_op jit(solution)/shard_map/pallas_call | solution.py:699
  38.6 0.8 %shard_map.96 = (f32[3,4,96,128]{3,2,1,0:T(8,128)}, f32[2,4,512]{2,1,0:T(4,128)}) custom-call(f32[3,4,96,128]{3,2,1,0:T(8,128)S(1)} %get-tuple-element.4.field, f32[2,4,512]{2,1,0:T(4,128)S(1)} %get-tuple-element.5.far), custom_call_target="tpu_custom_call" | custom-call | tf_op jit(solution)/shard_map/pallas_call | solution.py:750

commit v5 on v4

--- a/solution.py
+++ b/solution.py
@@ -393,11 +393,26 @@
                 rows = pl.ds(group * 24, 24)
                 inn[rows, f * LANES : (f + 1) * LANES] += real * part + imag * pltpu.roll(part, 64, 1)
 
+    def pack_corners(s, par):
+        left_col = jnp.zeros((CH, LANES), F32)
+        right_col = jnp.zeros((CH, LANES), F32)
+        for cut in range(NCH):
+            z = pl.ds(cut * CH, CH)
+            left_col = put(left_col, eb[par, 0, LX - 1, z, :], 0, cut * 16)
+            right_col = put(right_col, eb[par, 1, 0, z, :], LANES - 1, cut * 16)
+        tl[s] = left_col
+        tr[s] = right_col
+
+    def send_corners(s):
+        pl.when(has_r & has_d)(lambda: l2_copy(s).start())
+        pl.when(has_l & has_u)(lambda: r2_copy(s).start())
+
     loads[0].wait()
     loads[1].wait()
     for cut in range(NCH - 1, -1, -1):
         outer_h(0, 0, cut)
     loads[2].wait()
+    pack_corners(0, 0)
     greeted = (
         22
         + has_l.astype(jnp.int32)
@@ -406,6 +421,7 @@
         + (has_r & has_d).astype(jnp.int32)
     )
     pl.semaphore_wait(barrier, greeted)
+    send_corners(0)
 
     @pl.when(has_l)
     def _():
@@ -416,18 +432,6 @@
     def _():
         for cut in range(NCH - 1, -1, -1):
             xh_copy(0, cut).start()
-
-    def send_corners(s, par):
-        left_col = jnp.zeros((CH, LANES), F32)
-        right_col = jnp.zeros((CH, LANES), F32)
-        for cut in range(NCH):
-            z = pl.ds(cut * CH, CH)
-            left_col = put(left_col, eb[par, 0, LX - 1, z, :], 0, cut * 16)
-            right_col = put(right_col, eb[par, 1, 0, z, :], LANES - 1, cut * 16)
-        tl[s] = left_col
-        tr[s] = right_col
-        pl.when(has_r & has_d)(lambda: l2_copy(s).start())
-        pl.when(has_l & has_u)(lambda: r2_copy(s).start())
 
     def put_low(pack, par, x):
         for cut in range(NCH):
@@ -458,7 +462,6 @@
         sr[s] = put_high(put_high(put_high(sr[s], par, 3), par, 0, done), par, 2, done)
         pl.when(has_u)(lambda: r1_copy(s).start())
 
-    send_corners(0, 0)
     loads[3].wait()
     early_pack(0, 0)
 
@@ -593,7 +596,8 @@
                 next_high(cut + 1)
         fix_outer(s, par, 0)
         if more:
-            send_corners(s + 1, 1 - par)
+            pack_corners(s + 1, 1 - par)
+            send_corners(s + 1)
         next_low(0)
         next_high(1)
         next_high(0)

time: 39.6 us -> 38.8 us (0.980)
  Pallas kernels: 38.8 us -> 38 us
    pallas_call x1, Pallas kernels: 38 us -> 37.1 us  [local(): pl.pallas_call(kernel, out_shape=(jax.ShapeDtypeStruct(state, F32), jax.S...]
where the time goes in v5:
time: 38.8 us; the launch traced here: 38.6 us
  Pallas kernels  38 us (98%)
  between operations  0.64 us (2%)
    pallas_call x1, Pallas kernels, local(): pl.pallas_call(kernel, out_shape=(jax.ShapeDtypeStruct(state, F32), jax.S...  37.1 us
    pallas_call x1, Pallas kernels, local(): pl.pallas_call(store, out_shape=(jax.ShapeDtypeStruct(state, F32), jax.Sh...  0.84 us

profile of v5, /device:TPU:0, one launch (start us, length us, event | category | flops | bytes accessed | tf_op | source)
XLA Modules:
  0.0 38.6 jit_solution(754243528382263414)
XLA Ops:
  0.6 37.1 %shard_map.95 = (f32[3,4,96,128]{3,2,1,0:T(8,128)S(1)}, f32[2,4,512]{2,1,0:T(4,128)S(1)}) custom-call(f32[3,4,96,128]{3,2,1,0:T(8,128)} %e_in.1, f32[3,4,96,128]{3,2,1,0:T(8,128)} %h_in.1, f32[3,4,96,128]{3,2,1,0:T(8,128)} %p_in.1, f32[3,4,96,128]{3,2,1,0:T(8,128)} %j_in.1, f32[4,96,128]{2,1,0:T(8,128)} %w_in.1, s32[4,96,128]{2,1,0:T(8,128)} %g_in.1, ...), custom_call_target="tpu_custom_call" | custom-call | tf_op jit(solution)/shard_map/pallas_call | solution.py:703
  37.8 0.8 %shard_map.96 = (f32[3,4,96,128]{3,2,1,0:T(8,128)}, f32[2,4,512]{2,1,0:T(4,128)}) custom-call(f32[3,4,96,128]{3,2,1,0:T(8,128)S(1)} %get-tuple-element.4.field, f32[2,4,512]{2,1,0:T(4,128)S(1)} %get-tuple-element.5.far), custom_call_target="tpu_custom_call" | custom-call | tf_op jit(solution)/shard_map/pallas_call | solution.py:754
